TPU v7x, 128 devices: a whole 4x4x4 slice. The times are simulated.
128 devices in a mesh: ang: 16 (over z_lo, x, core), kslab: 8 (over z_hi, y).
Axes of the slice: x: 4, y: 4, z: 4 (z_hi: 2, z_lo: 2; z = z_hi * 2 + z_lo), core: 2. Of those that a mesh axis runs over, the one named last changes fastest.
Arguments:
- amplitude: bfloat16 [256, 112, 8, 2048], P('ang', None, 'kslab'), may hold values from -6 to 6
- ps_form: bfloat16 [2048, 896], replicated, may hold values from -0.125 to 0.125
- kgrid: float32 [8], replicated, may hold values from 0.1 to 3
- l_atom: int32 [112], replicated, may hold values from 0 to 7
- l_ps: int32 [112], replicated, may hold values from 0 to 7
- sixj: float32 [8, 12, 8, 8], replicated, may hold values from -0.5 to 0.5
Outputs:
- kernel: float32 [112, 8, 8, 896], P('ang', 'kslab')
All inputs are finite; a program needn't handle non-finite values.
Results may differ from a plain program's by a relative error of at most 0.0003.
Values sent between devices are 32-bit elements; how exact they have to be, the bound alone decides.
No kernel may reach another device: no remote copies, remote signals or barrier semaphores. Data moves between devices by JAX's collectives and lax.ppermute only.
A program may use at most 128 MiB of HBM per device.

v0:
```python
import jax
import jax.numpy as jnp
from jax import lax
from jax.sharding import PartitionSpec as P


def legendre_table(first_row, row_count, total_points, degrees):
    positions = (first_row + jnp.arange(row_count)).astype(jnp.float32)
    angles = jnp.pi * (positions + 0.5) / total_points
    grid_nodes = jnp.cos(angles)
    grid_weights = jnp.pi / total_points * jnp.sin(angles)
    series = [jnp.ones_like(grid_nodes), grid_nodes]
    for degree in range(1, degrees - 1):
        series.append(
            ((2 * degree + 1) * grid_nodes * series[-1] - degree * series[-2]) / (degree + 1)
        )
    return (grid_nodes, grid_weights[None, :] * jnp.stack(series[:degrees]))


def recouple(values, channel_first, j_first, j_count, l_atom, l_ps, sixj, kpoints):
    channel_count = values.shape[0]
    levels = jnp.arange(sixj.shape[2], dtype=jnp.int32)
    atom_levels = lax.dynamic_slice_in_dim(l_atom, channel_first, channel_count)
    onehot_atom = (atom_levels[:, None] == levels[None, :]).astype(jnp.float32)
    onehot_ps = (l_ps[:, None] == levels[None, :]).astype(jnp.float32)
    table = lax.dynamic_slice_in_dim(sixj, j_first, j_count, 0)
    coupling = jnp.einsum(
        "jlxy,ax,by->ajlb", table, onehot_atom, onehot_ps, precision=lax.Precision.HIGHEST
    )
    widened = jnp.repeat(coupling, kpoints, axis=3)
    return jnp.einsum("ajlc,alkc->ajkc", widened, values, precision=lax.Precision.HIGHEST)


def local(amplitude, ps_form, kgrid, l_atom, l_ps, sixj):
    grid_count, channels, slab_points, radial = amplitude.shape
    columns = ps_form.shape[1]
    kpoints = kgrid.shape[0]
    ps_channels = columns // kpoints
    degrees = sixj.shape[1]
    total_j = sixj.shape[0]
    ang_size = lax.axis_size("ang")
    slab_size = lax.axis_size("kslab")
    owned = channels // ang_size
    owned_first = lax.axis_index("ang") * owned
    j_local = total_j // slab_size
    j_first = lax.axis_index("kslab") * j_local
    grid_nodes, projector = legendre_table(
        lax.axis_index("ang") * grid_count, grid_count, grid_count * ang_size, degrees
    )
    krow = lax.dynamic_slice_in_dim(kgrid, lax.axis_index("kslab") * slab_points, slab_points)[
        None, :, None
    ]
    kcol = jnp.tile(kgrid, ps_channels)[None, None, :]
    qinverse = 1.0 / (
        1.0 + krow * krow + kcol * kcol - 2.0 * grid_nodes[:, None, None] * krow * kcol
    )
    intersection = jnp.dot(
        amplitude.reshape(-1, radial), ps_form, preferred_element_type=jnp.float32
    )
    intersection = intersection.reshape(
        grid_count, lax.axis_size("ang") * owned, slab_points, columns
    )
    integrand = intersection * qinverse[:, None]
    summed = lax.psum_scatter(
        jnp.einsum("lg,gakc->alkc", projector, integrand, precision=lax.Precision.HIGHEST),
        "ang",
        scatter_dimension=0,
        tiled=True,
    )
    return recouple(
        lax.all_gather(summed, "kslab", axis=2, tiled=True),
        owned_first,
        j_first,
        j_local,
        l_atom,
        l_ps,
        sixj,
        kpoints,
    )


def solution(mesh):
    in_specs = (P("ang", None, "kslab", None), P(), P(), P(), P(), P())
    out_specs = P("ang", "kslab", None, None)
    return jax.shard_map(local, mesh=mesh, in_specs=in_specs, out_specs=out_specs, check_vma=False)
```

profile of v0, /device:TPU:0, one launch (start us, length us, event | category | flops | bytes accessed | tf_op | source)
XLA Modules:
  0.0 186.1 jit_solution(9028260817376288900)
XLA Ops:
  6.5 0.1 broadcast_multiply_fusion.1
  6.6 0.1 broadcast_multiply_fusion.3
  6.7 0.1 broadcast_multiply_fusion.5
  6.7 0.1 subtract_multiply_fusion
  6.8 0.1 multiply_cosine_fusion
  6.9 0.1 broadcast_multiply_fusion.7
  6.9 1.2 dynamic_slice.9
  10.2 0.7 tile.2
  10.8 0.1 broadcast_in_dim_tile.3
  11.0 0.1 subtract_divide_fusion
  11.0 21.4 %fusion = f32[16,112,896]{2,0,1:T(8,128)} fusion(bf16[16,112,2048]{2,1,0:T(8,128)(2,1)} %bitcast.36, bf16[2048,896]{1,0:T(8,128)(2,1)} %param.7), kind=kOutput, calls=%fused_computation | convolution fusion | flops 6576668672 | bytes 17432576 | tf_op jit(solution)/shard_map/dot_general | solution.py:57
  32.5 9.5 %fusion.6 = f32[112,12,1,896]{3,1,0,2:T(8,128)} fusion(f32[16,112,896]{2,0,1:T(8,128)} %fusion, f32[16,896]{1,0:T(8,128)S(1)} %subtract_divide_fusion, f32[12,16]{1,0:T(8,128)S(1)} %stack.2, f32[16]{0:T(128)S(1)} %get-tuple-element.9), kind=kOutput, calls=%fused_computation.7 | convolution fusion | flops 232816832 | bytes 11297600 | tf_op jit(solution)/shard_map/lg,gakc->alkc/dot_general | solution.py:65
  42.1 0.2 all-gather.2.cloned.1.call-start
  42.3 73.4 %reduce-scatter.2.cloned.1.call-done = f32[7,12,1,896]{3,1,0,2:T(8,128)} async-done(((f32[112,12,1,896]{3,1,0,2:T(8,128)}), f32[7,12,1,896]{3,1,0,2:T(8,128)}) %reduce-scatter.2.cloned.1.call-update) | async-done | bytes 301072 | tf_op jit(solution)/shard_map/reduce_scatter | solution.py:64
  115.6 1.8 copy.9
  117.5 0.1 dynamic_slice.10
  117.6 0.2 fusion.9
  117.8 0.1 copy.13
  117.9 0.2 fusion.18
  118.1 3.3 %broadcast_in_dim.4 = f32[7,12,112,8]{3,2,0,1:T(8,128)} broadcast(f32[7,12,112]{2,0,1:T(8,128)S(1)} %fusion.18), dimensions={0,1,2} | broadcast | bytes 338688 | tf_op jit(solution)/shard_map/broadcast_in_dim | solution.py:30
  121.4 4.1 %broadcast_in_dim.5 = f32[7,12,896]{2,0,1:T(8,128)S(1)} reshape(f32[7,12,112,8]{3,2,0,1:T(8,128)} %broadcast_in_dim.4) | data formatting | bytes 602112 | tf_op jit(solution)/shard_map/broadcast_in_dim | solution.py:30
  125.5 50.9 %all-gather.2.cloned.1.call-done = f32[7,12,8,896]{3,0,1,2:T(8,128)} async-done(((f32[7,12,1,896]{3,0,1,2:T(8,128)}), f32[7,12,8,896]{3,0,1,2:T(8,128)}) %all-gather.2.cloned.1.call-update) | async-done | bytes 2408464 | tf_op jit(solution)/shard_map/all_gather | solution.py:71
  176.5 2.1 %multiply_reduce_fusion = f32[7,896,8]{1,0,2:T(8,128)S(1)} fusion(f32[7,12,8,896]{3,0,1,2:T(8,128)} %all-gather.2.cloned.1.call-done, f32[7,896,12]{1,0,2:T(8,128)S(1)} %bitcast.35), kind=kLoop, calls=%fused_computation.6 | loop fusion | flops 1154048 | bytes 2910208
  178.5 0.7 copy.32
  (14 shorter events, 0.2 us)
Async XLA Ops:
  6.5 111.1 %copy-start = (f32[8,12,8,8]{1,3,2,0:T(8,128)S(1)}, f32[8,12,8,8]{1,3,2,0:T(8,128)}, u32[]{:S(2)}) copy-start(f32[8,12,8,8]{1,3,2,0:T(8,128)} %param.11) | copy-start | bytes 73732
  6.5 109.1 %reduce-scatter.2.cloned.1.call-start = ((), (), s32[]{:S(2)}) async-start(), calls=%async_computation.1 | async-start | bytes 6823936 | tf_op jit(solution)/shard_map/reduce_scatter | solution.py:64
  42.0 75.5 %copy-start.2 = (s32[112]{0:T(128)S(1)}, s32[112]{0:T(128)}, u32[]{:S(2)}) copy-start(s32[112]{0:T(128)} %param.9) | copy-start | bytes 1348
  42.0 75.9 %copy-start.1 = (s32[112]{0:T(128)S(1)}, s32[112]{0:T(128)}, u32[]{:S(2)}) copy-start(s32[112]{0:T(128)} %param.10) | copy-start | bytes 1348
  42.1 134.4 %all-gather.2.cloned.1.call-start = ((), (), s32[]{:S(2)}) async-start(), calls=%async_computation.2 | async-start | bytes 3096576 | tf_op jit(solution)/shard_map/all_gather | solution.py:71
Sparse Core Ops, SparseCore 0:
  42.2 73.4 reduce-scatter.1
  118.0 58.4 all-gather.1
where the time goes:
time: 187 us; the launch traced here: 186 us
  waiting for transfers between devices  124 us (66%)
  matrix products  31.3 us (17%)
  between operations  15.4 us (8%)
  local copies, waits for them, and re-layouts  12.2 us (7%)
  other arithmetic  2.6 us (1%)
    reduce_scatter x1, waiting for transfers between devices, local(): lax.psum_scatter(jnp.einsum('lg,gakc->alkc', projector, integrand, precis...  73.4 us
    all_gather x1, waiting for transfers between devices, local(): lax.all_gather(summed, 'kslab', axis=2, tiled=True)  50.9 us
    dot_general x1, matrix products, local(): jnp.dot(amplitude.reshape(-1, radial), ps_form, preferred_element_type=jn...  21.4 us
    dot_general x1, matrix products, local(): jnp.einsum('lg,gakc->alkc', projector, integrand, precision=lax.Precision...  9.49 us
    broadcast_in_dim x2, local copies, waits for them, and re-layouts, recouple(): widened = jnp.repeat(coupling, kpoints, axis=3)  7.37 us
  transfers between devices with their start and end apart: 2, of which 2 were waited for; matrix products, arithmetic and copies ran while one was open for 4% of the time, Pallas kernels for 0%

commit v1 on v0

v1 whole, which is shorter than its diff:
```python
import functools
import math

import jax
import jax.numpy as jnp
from jax import lax
from jax.experimental import pallas as pl
from jax.experimental.pallas import tpu as pltpu
from jax.sharding import Mesh, PartitionSpec as P

F32 = jnp.float32
BF16 = jnp.bfloat16
LANES = 128
SUB = 8


def one_hot_lanes(rows, lanes, row_of, lane_of, dtype):
    r = lax.broadcasted_iota(jnp.int32, (rows, lanes), 0)
    c = lax.broadcasted_iota(jnp.int32, (rows, lanes), 1)
    return (row_of(r) == lane_of(c)).astype(dtype)


def build_tables(dims, place, kgrid, lps_ref, six_ref, r1_ref, pq_ref, x3_ref, w_ref):
    grid_count, total_points, degrees, levels, kpoints, ps_channels, columns = dims
    shape = (grid_count, LANES)
    first = place[0] * grid_count
    position = (first + lax.broadcasted_iota(jnp.int32, shape, 0)).astype(F32)
    theta = math.pi * (position + 0.5) / total_points
    node = jnp.cos(theta)
    weight = (math.pi / total_points) * jnp.sin(theta)
    kidx = lax.broadcasted_iota(jnp.int32, shape, 1) % kpoints
    kcol = jnp.zeros(shape, F32)
    for q in range(kpoints):
        kcol = jnp.where(kidx == q, kgrid[q], kcol)
    krow = kgrid[place[1]]
    qinverse = 1.0 / (1.0 + krow * krow + kcol * kcol - 2.0 * node * krow * kcol)
    scale = weight * qinverse
    series = [jnp.ones(shape, F32), node]
    for degree in range(1, degrees - 1):
        series.append(((2 * degree + 1) * node * series[-1] - degree * series[-2]) / (degree + 1))
    for degree in range(degrees):
        pq_ref[pl.ds(degree * grid_count, grid_count), :] = series[degree] * scale
    half = levels * kpoints
    spread = one_hot_lanes(levels, LANES, lambda r: r, lambda c: (c % half) // kpoints, F32)
    r1_ref[...] = jnp.dot(six_ref[...], spread, precision=lax.Precision.HIGHEST, preferred_element_type=F32)
    low = lax.broadcasted_iota(jnp.int32, (2 * SUB, LANES), 1) < half
    stride = degrees * levels
    for level in range(levels):
        coef = [r1_ref[pl.ds(degree * levels + level, SUB, stride=stride), :] for degree in range(degrees)]
        for pair in range(grid_count // 2):
            both = []
            for g in (2 * pair, 2 * pair + 1):
                acc = None
                for degree in range(degrees):
                    row = jnp.broadcast_to(pq_ref[pl.ds(degree * grid_count + g, 1), :], (SUB, LANES))
                    term = coef[degree] * row
                    acc = term if acc is None else acc + term
                both.append(acc)
            value = jnp.concatenate(both, axis=0)
            hi = value.astype(BF16).astype(F32)
            rest = value - hi
            mid = rest.astype(BF16).astype(F32)
            tail = rest - mid
            rows = pl.ds((level * grid_count + 2 * pair) * SUB, 2 * SUB)
            x3_ref[rows, 0:LANES] = jnp.where(low, hi, mid).astype(BF16)
            x3_ref[rows, LANES:2 * LANES] = jnp.where(low, tail, 0.0).astype(BF16)
    rep = one_hot_lanes(ps_channels, columns, lambda r: r, lambda c: c // kpoints, F32)
    level_of = jnp.dot(lps_ref[...].astype(F32), rep, preferred_element_type=F32)
    code = level_of.astype(jnp.int32) * kpoints + lax.broadcasted_iota(jnp.int32, (1, columns), 1) % kpoints
    r = lax.broadcasted_iota(jnp.int32, (2 * LANES, columns), 0)
    pick = ((r % half == code) & (r < 3 * half)).astype(F32).astype(BF16)
    w_ref[...] = jnp.dot(x3_ref[...], pick, preferred_element_type=F32)


def kernel_body(dims, geometry, place, l_atom, kgrid, lps_ref, six_ref, a_ref, ps_ref, send_ref, keep_ref,
                i_ref, w_ref, r1_ref, pq_ref, x3_ref):
    grid_count, total_points, degrees, levels, kpoints, ps_channels, columns = dims
    channels, owned, groups, block = geometry
    step = pl.program_id(0)

    @pl.when(step == 0)
    def _():
        build_tables(dims, place, kgrid, lps_ref, six_ref, r1_ref, pq_ref, x3_ref, w_ref)

    rows = block * channels
    product = jnp.dot(a_ref[...].reshape(rows, a_ref.shape[-1]), ps_ref[...], preferred_element_type=F32)
    for t in range(columns // LANES):
        i_ref[t, pl.ds(pl.multiple_of(step * rows, rows), rows), :] = product[:, t * LANES:(t + 1) * LANES]

    @pl.when(step == pl.num_programs(0) - 1)
    def _():
        tiles = columns // LANES
        chunk = tiles * SUB
        for slot, out_ref in ((0, send_ref), (1, keep_ref)):
            core = place[2] if slot == 1 else 1 - place[2]

            def group(d, carry):
                for r in range(owned):
                    a = d * (2 * owned) + core * owned + r
                    base = l_atom[a] * (grid_count * SUB)
                    acc = [None] * tiles
                    for g in range(grid_count):
                        for t in range(tiles):
                            cols = slice(t * LANES, (t + 1) * LANES)
                            coef = w_ref[pl.ds(pl.multiple_of(base + g * SUB, SUB), SUB), cols]
                            row = i_ref[t, pl.ds(g * channels + a, SUB, stride=0), :]
                            term = coef * row
                            acc[t] = term if acc[t] is None else acc[t] + term
                    for t in range(tiles):
                        out_ref[pl.ds(d * (SUB * chunk) + t * SUB + r, SUB, stride=chunk), :] = acc[t]
                return carry

            lax.fori_loop(0, groups, group, 0)


def partial_kernel(amplitude, ps_form, kgrid, l_atom, l_ps, sixj, place, total_points):
    grid_count, channels, radial = amplitude.shape
    columns = ps_form.shape[1]
    kpoints = kgrid.shape[0]
    total_j, degrees, levels, _ = sixj.shape
    ps_channels = l_ps.shape[0]
    owned = channels * grid_count // total_points
    groups = channels // (2 * owned)
    block = 4
    dims = (grid_count, total_points, degrees, levels, kpoints, ps_channels, columns)
    geometry = (channels, owned, groups, block)
    out = jax.ShapeDtypeStruct((groups * total_j * SUB * columns // LANES, LANES), F32)
    smem = pl.BlockSpec(memory_space=pltpu.SMEM)

    def whole(shape):
        return pl.BlockSpec(shape, lambda i: (0,) * len(shape), pipeline_mode=pl.Buffered(1))

    six = sixj.reshape(-1, levels)
    return pl.pallas_call(
        functools.partial(kernel_body, dims, geometry),
        grid=(grid_count // block,),
        in_specs=[
            smem, smem, smem,
            whole((1, ps_channels)),
            whole(six.shape),
            pl.BlockSpec((block, channels, radial), lambda i: (i, 0, 0)),
            whole(ps_form.shape),
        ],
        out_specs=[pl.BlockSpec(out.shape, lambda i: (0, 0))] * 2,
        out_shape=[out, out],
        scratch_shapes=[
            pltpu.VMEM((columns // LANES, grid_count * channels, LANES), F32),
            pltpu.VMEM((levels * grid_count * SUB, columns), F32),
            pltpu.VMEM((six.shape[0], LANES), F32),
            pltpu.VMEM((degrees * grid_count, LANES), F32),
            pltpu.VMEM((levels * grid_count * SUB, 2 * LANES), BF16),
        ],
        compiler_params=pltpu.CompilerParams(
            dimension_semantics=("arbitrary",), vmem_limit_bytes=56 * 1024 * 1024
        ),
        name="recoupled_partials",
    )(place, l_atom, kgrid, l_ps.reshape(1, -1), six, amplitude, ps_form)


def local(amplitude, ps_form, kgrid, l_atom, l_ps, sixj):
    grid_count, channels, slab_points, radial = amplitude.shape
    columns = ps_form.shape[1]
    total_j = sixj.shape[0]
    ang_size = lax.axis_size(("zl", "x", "core"))
    owned = channels // ang_size
    groups = ang_size // 2
    place = jnp.stack(
        [lax.axis_index(("zl", "x", "core")), lax.axis_index(("zh", "y")), lax.axis_index("core")]
    ).astype(jnp.int32)
    send, keep = partial_kernel(
        amplitude.reshape(grid_count, channels, radial), ps_form, kgrid, l_atom, l_ps, sixj, place,
        grid_count * ang_size,
    )
    mine = keep + lax.ppermute(send, "core", [(0, 1), (1, 0)])
    tiles = columns // LANES
    mine = mine.reshape(groups * total_j, tiles * SUB, LANES)
    got = lax.all_to_all(mine, ("zl", "x", "zh", "y"), split_axis=0, concat_axis=0, tiled=True)
    total = jnp.sum(got.reshape(groups, total_j, tiles, SUB, LANES), axis=0)
    return jnp.transpose(total[:, :, :owned], (2, 0, 1, 3)).reshape(owned, 1, total_j, columns)


def solution(mesh):
    fine = Mesh(mesh.devices.reshape(2, 4, 2, 2, 4), ("zl", "x", "core", "zh", "y"))
    ang, slab = ("zl", "x", "core"), ("zh", "y")
    in_specs = (P(ang, None, slab, None), P(), P(), P(), P(), P())
    out_specs = P(ang, slab, None, None)
    return jax.shard_map(local, mesh=fine, in_specs=in_specs, out_specs=out_specs, check_vma=False)
```

time: 187 us -> 69.9 us (0.37)
  waiting for transfers between devices: 124 us -> 3.99 us
  blocking collectives: 0 us -> 37.4 us
  matrix products: 31.3 us -> 0 us
  Pallas kernels: 0 us -> 22.4 us
  between operations: 15.4 us -> 0.02 us
  local copies, waits for them, and re-layouts: 12.2 us -> 2.9 us
    reduce_scatter x1 -> x0, waiting for transfers between devices: 73.4 us -> none  [local(): lax.psum_scatter(jnp.einsum('lg,gakc->alkc', projector, integrand, precis...]
    all_gather x1 -> x0, waiting for transfers between devices: 50.9 us -> none  [local(): lax.all_gather(summed, 'kslab', axis=2, tiled=True)]
    all_to_all x0 -> x1, blocking collectives: none -> 37.4 us  [local(): lax.all_to_all(mine, ('zl', 'x', 'zh', 'y'), split_axis=0, concat_axis=0,...]
    dot_general x4 -> x0, matrix products: 31.3 us -> none  [the longest x1 21.4 us: local(): jnp.dot(amplitude.reshape(-1, radial), ps_form, preferred_element_type=jn...]
    pallas_call x0 -> x1, Pallas kernels: none -> 22.4 us  [partial_kernel(): pl.pallas_call(functools.partial(kernel_body, dims, geometry), grid=(grid...]
    broadcast_in_dim x2 -> x0, local copies, waits for them, and re-layouts: 7.37 us -> none  [recouple(): widened = jnp.repeat(coupling, kpoints, axis=3)]
    ppermute x0 -> x1, waiting for transfers between devices: none -> 3.99 us  [local(): mine = keep + lax.ppermute(send, 'core', [(0, 1), (1, 0)])]
    unnamed x6 -> x1, local copies, waits for them, and re-layouts: 0.01 us -> 2.17 us
  transfers between devices with their start and end apart: 2 -> 1, of which waited for: 2 -> 1; matrix products, arithmetic and copies ran while one was open for 4% -> 0% of each run, Pallas kernels for 0% -> 0%
where the time goes in v1:
time: 69.9 us; the launch traced here: 69.2 us
  blocking collectives  37.4 us (54%)
  Pallas kernels  22.4 us (32%)
  waiting for transfers between devices  3.99 us (6%)
  local copies, waits for them, and re-layouts  2.9 us (4%)
  other arithmetic  2.49 us (4%)
    all_to_all x1, blocking collectives, local(): lax.all_to_all(mine, ('zl', 'x', 'zh', 'y'), split_axis=0, concat_axis=0,...  37.4 us
    pallas_call x1, Pallas kernels, partial_kernel(): pl.pallas_call(functools.partial(kernel_body, dims, geometry), grid=(grid...  22.4 us
    ppermute x1, waiting for transfers between devices, local(): mine = keep + lax.ppermute(send, 'core', [(0, 1), (1, 0)])  3.99 us
    unnamed x1, local copies, waits for them, and re-layouts  2.17 us
    add x1, other arithmetic, local(): mine = keep + lax.ppermute(send, 'core', [(0, 1), (1, 0)])  1.74 us
  transfers between devices with their start and end apart: 1, of which 1 were waited for; matrix products, arithmetic and copies ran while one was open for 0% of the time, Pallas kernels for 0%

profile of v1, /device:TPU:0, one launch (start us, length us, event | category | flops | bytes accessed | tf_op | source)
XLA Modules:
  0.0 69.2 jit_solution(16644169598211542033)
XLA Ops:
  0.0 2.2 %copy.9 = f32[8,12,8,8]{3,2,1,0:T(8,128)} copy(f32[8,12,8,8]{1,3,2,0:T(8,128)} %param.11) | data formatting | bytes 49152 | tf_op args[5]
  2.2 0.7 pad_add_fusion.place
  2.8 22.4 %recoupled_partials.1 = (f32[3584,128]{1,0:T(8,128)}, f32[3584,128]{1,0:T(8,128)}) custom-call(s32[3]{0:T(128)} %pad_add_fusion.place, s32[112]{0:T(128)} %l_atom.1, f32[8]{0:T(128)} %kgrid.1, s32[1,112]{1,0:T(1,128)} %bitcast.19, f32[768,8]{1,0:T(8,128)} %bitcast.18, bf16[16,112,2048]{2,1,0:T(8,128)(2,1)} %bitcast.16, bf16[2048,896]{1,0:T(8,128)(2,1)} %ps_ref.1), custom_call_target="tpu_custom_call" | custom-call | tf_op jit(solution)/shard_map/recoupled_partials/pallas_call | solution.py:134
  25.2 0.0 collective-permute-start
  25.2 4.0 %collective-permute-done = f32[3584,128]{1,0:T(8,128)S(1)} collective-permute-done((f32[3584,128]{1,0:T(8,128)}, f32[3584,128]{1,0:T(8,128)S(1)}, u32[]{:S(2)}, u32[]{:S(2)}) %collective-permute-start) | collective-permute-done | bytes 1835040 | tf_op jit(solution)/shard_map/ppermute | solution.py:174
  29.2 1.7 %add.15 = f32[3584,128]{1,0:T(8,128)S(1)} add(f32[3584,128]{1,0:T(8,128)} %get-tuple-element.7, f32[3584,128]{1,0:T(8,128)S(1)} %collective-permute-done) | non-fusion elementwise | flops 458752 | bytes 5505024 | tf_op jit(solution)/shard_map/add | solution.py:174
  30.9 37.4 %all_to_all.5 = f32[64,56,128]{2,1,0:T(8,128)S(1)} all-to-all(f32[64,56,128]{2,1,0:T(8,128)S(1)} %bitcast.17), channel_id=1, replica_groups=mesh['zl'=2,'x'=4,'core'=2,'zh'=2,'y'=4] {'zl','x','zh','y'}, dimensions={0} | all-to-all | bytes 3670016 | tf_op jit(solution)/shard_map/all_to_all | solution.py:177
  68.3 0.1 reduce_sum.9
  68.5 0.7 %copy.13 = f32[7,8,7,128]{3,1,2,0:T(8,128)} copy(f32[7,8,7,128]{3,0,2,1:T(8,128)S(1)} %slice_bitcast_fusion) | data formatting | bytes 401408 | tf_op jit(solution)/shard_map/transpose | solution.py:179
  (1 shorter events, 0.0 us)
Async XLA Ops:
  25.2 4.0 %collective-permute-start = (f32[3584,128]{1,0:T(8,128)}, f32[3584,128]{1,0:T(8,128)S(1)}, u32[]{:S(2)}, u32[]{:S(2)}) collective-permute-start(f32[3584,128]{1,0:T(8,128)} %get-tuple-element.8), channel_id=1, source_target_pairs={{0,8},{8,0},{1,9},{9,1},{2,10},{10,2},{3,11},{11,3},{4,12},{12,4},... | collective-permute-start | bytes 5505032 | tf_op jit(solution)/shard_map/ppermute | solution.py:174

commit v2 on v1

v2 whole, which is shorter than its diff:
```python
import functools
import math

import jax
import jax.numpy as jnp
from jax import lax
from jax.experimental import pallas as pl
from jax.experimental.pallas import tpu as pltpu
from jax.sharding import Mesh, PartitionSpec as P

F32 = jnp.float32
BF16 = jnp.bfloat16
LANES = 128
SUB = 8
CHUNK = 2
BLOCK = 4
VMEM_LIMIT = 56 * 1024 * 1024


def iota(shape, axis):
    return lax.broadcasted_iota(jnp.int32, shape, axis)


def build_tables(dims, place, kgrid, lps_ref, six_ref, r1_ref, pq_ref, x3_ref, w_ref):
    grid_count, total_points, degrees, levels, kpoints, ps_channels, columns = dims
    shape = (grid_count, LANES)
    position = (place[0] * grid_count + iota(shape, 0)).astype(F32)
    theta = math.pi * (position + 0.5) / total_points
    node = jnp.cos(theta)
    weight = (math.pi / total_points) * jnp.sin(theta)
    kidx = iota(shape, 1) % kpoints
    kcol = jnp.zeros(shape, F32)
    for q in range(kpoints):
        kcol = jnp.where(kidx == q, kgrid[q], kcol)
    krow = kgrid[place[1]]
    qinverse = 1.0 / (1.0 + krow * krow + kcol * kcol - 2.0 * node * krow * kcol)
    scale = weight * qinverse
    series = [jnp.ones(shape, F32), node]
    for degree in range(1, degrees - 1):
        series.append(((2 * degree + 1) * node * series[-1] - degree * series[-2]) / (degree + 1))
    for degree in range(degrees):
        pq_ref[pl.ds(degree * grid_count, grid_count), :] = series[degree] * scale
    half = levels * kpoints
    pad = 2 * SUB
    eye = (iota((pad, degrees), 0) == iota((pad, degrees), 1)).astype(F32)
    turned = lax.dot_general(
        eye, six_ref[...], (((1,), (1,)), ((), ())), precision=lax.Precision.HIGHEST, preferred_element_type=F32
    )
    pairs = levels * levels
    turned = jnp.concatenate([turned[:, j * pairs:(j + 1) * pairs] for j in range(SUB)], axis=0)
    spread_shape = (pairs, levels * LANES)
    source = iota(spread_shape, 0)
    target = iota(spread_shape, 1)
    wanted = (target // LANES) * levels + (target % half) // kpoints
    spread = (source == wanted).astype(F32)
    expanded = jnp.dot(turned, spread, precision=lax.Precision.HIGHEST, preferred_element_type=F32)
    for level in range(levels):
        r1_ref[level] = expanded[:, level * LANES:(level + 1) * LANES]
    low = iota((2 * SUB, LANES), 1) < half
    for level in range(levels):
        coef = [r1_ref[level, pl.ds(degree, SUB, stride=pad), :] for degree in range(degrees)]
        for pair in range(grid_count // 2):
            both = []
            for g in (2 * pair, 2 * pair + 1):
                acc = None
                for degree in range(degrees):
                    row = pq_ref[pl.ds(degree * grid_count + g, SUB, stride=0), :]
                    term = coef[degree] * row
                    acc = term if acc is None else acc + term
                both.append(acc)
            value = jnp.concatenate(both, axis=0)
            hi = value.astype(BF16).astype(F32)
            rest = value - hi
            mid = rest.astype(BF16).astype(F32)
            tail = rest - mid
            rows = pl.ds((level * grid_count + 2 * pair) * SUB, 2 * SUB)
            x3_ref[rows, 0:LANES] = jnp.where(low, hi, mid).astype(BF16)
            x3_ref[rows, LANES:2 * LANES] = jnp.where(low, tail, 0.0).astype(BF16)
    rep_shape = (ps_channels, columns)
    rep = (iota(rep_shape, 0) == iota(rep_shape, 1) // kpoints).astype(F32)
    level_of = jnp.dot(lps_ref[...].astype(F32), rep, preferred_element_type=F32)
    code = level_of.astype(jnp.int32) * kpoints + iota((1, columns), 1) % kpoints
    r = iota((2 * LANES, columns), 0)
    pick = ((r % half == code) & (r < 3 * half)).astype(F32).astype(BF16)
    w_ref[...] = jnp.dot(x3_ref[...], pick, preferred_element_type=F32)


def recouple_group(geometry, l_atom, i_ref, w_ref, out_ref, first_tile, count, core, d):
    grid_count, channels, owned, groups, tiles = geometry
    rows = tiles * owned
    for r in range(owned):
        a = (2 * d + core) * owned + r
        base = l_atom[a] * (grid_count * SUB)
        acc = [None] * count
        for g in range(grid_count):
            for t in range(count):
                lo = (first_tile + t) * LANES
                coef = w_ref[pl.ds(pl.multiple_of(base + g * SUB, SUB), SUB), lo:lo + LANES]
                term = coef * i_ref[t, pl.ds(g * channels + a, SUB, stride=0), :]
                acc[t] = term if acc[t] is None else acc[t] + term
        for t in range(count):
            out_ref[pl.ds(d * (SUB * rows) + (first_tile + t) * owned + r, SUB, stride=rows), :] = acc[t]


def tile_chunks(tiles):
    return [(t, min(CHUNK, tiles - t)) for t in range(0, tiles, CHUNK)]


def first_body(dims, geometry, l_atom, kgrid, lps_ref, six_ref, a_hbm, ps_hbm, *rest):
    grid_count, channels, owned, groups, tiles = geometry
    chunks = tile_chunks(tiles)
    send_ref, w_ref = rest[:2]
    i_refs = rest[2:2 + len(chunks)]
    a_ref, ps_ref, r1_ref, pq_ref, x3_ref, a_sems, ps_sem = rest[2 + len(chunks):]
    core = lax.axis_index("core")
    ang = (lax.axis_index("zl") * lax.axis_size("x") + lax.axis_index("x")) * lax.axis_size("core") + core
    slab = lax.axis_index("zh") * lax.axis_size("y") + lax.axis_index("y")

    def copy_a(m):
        block = pl.ds(m * BLOCK, BLOCK)
        return pltpu.make_async_copy(a_hbm.at[block], a_ref.at[block], a_sems.at[m])

    copy_ps = pltpu.make_async_copy(ps_hbm, ps_ref, ps_sem)
    copy_ps.start()
    steps = grid_count // BLOCK
    for m in range(steps):
        copy_a(m).start()
    build_tables(dims, (ang, slab), kgrid, lps_ref, six_ref, r1_ref, pq_ref, x3_ref, w_ref)
    copy_ps.wait()
    rows = BLOCK * channels
    radial = a_ref.shape[-1]
    per_step = groups // steps
    for n, (first_tile, count) in enumerate(chunks):
        def step(m, carry, n=n, first_tile=first_tile, count=count):
            if n == 0:
                copy_a(m).wait()
            left = a_ref[pl.ds(m * BLOCK, BLOCK)].reshape(rows, radial)
            product = jnp.dot(
                left, ps_ref[:, first_tile * LANES:(first_tile + count) * LANES], preferred_element_type=F32
            )
            if n > 0:
                for s in range(per_step):
                    recouple_group(
                        geometry, l_atom, i_refs[n - 1], w_ref, send_ref, *chunks[n - 1], 1 - core, m * per_step + s
                    )
            for t in range(count):
                i_refs[n][t, pl.ds(pl.multiple_of(m * rows, rows), rows), :] = product[:, t * LANES:(t + 1) * LANES]
            return carry

        lax.fori_loop(0, steps, step, 0)

    def last(d, carry):
        recouple_group(geometry, l_atom, i_refs[-1], w_ref, send_ref, *chunks[-1], 1 - core, d)
        return carry

    lax.fori_loop(0, groups, last, 0)


def second_body(geometry, l_atom, w_ref, *rest):
    groups, tiles = geometry[3:]
    chunks = tile_chunks(tiles)
    keep_ref = rest[-1]
    core = lax.axis_index("core")

    def group(d, carry):
        for n, chunk in enumerate(chunks):
            recouple_group(geometry, l_atom, rest[n], w_ref, keep_ref, *chunk, core, d)
        return carry

    lax.fori_loop(0, groups, group, 0)


def sum_body(owned, tiles, sources, total_j, got_ref, out_ref):
    rows = owned * tiles
    for r in range(owned):
        for t in range(tiles):
            acc = None
            for s in range(sources):
                part = got_ref[pl.ds(s * total_j * rows + t * owned + r, total_j, stride=rows), :]
                acc = part if acc is None else acc + part
            out_ref[r, :, t * LANES:(t + 1) * LANES] = acc


def local(amplitude, ps_form, kgrid, l_atom, l_ps, sixj):
    grid_count, channels, slab_points, radial = amplitude.shape
    columns = ps_form.shape[1]
    kpoints = kgrid.shape[0]
    total_j, degrees, levels, _ = sixj.shape
    ps_channels = l_ps.shape[0]
    ang_size = lax.axis_size(("zl", "x", "core"))
    owned = channels // ang_size
    groups = ang_size // 2
    tiles = columns // LANES
    dims = (grid_count, grid_count * ang_size, degrees, levels, kpoints, ps_channels, columns)
    geometry = (grid_count, channels, owned, groups, tiles)
    smem = pl.BlockSpec(memory_space=pltpu.SMEM)
    vmem = pl.BlockSpec(memory_space=pltpu.VMEM)
    hbm = pl.BlockSpec(memory_space=pl.ANY)
    params = pltpu.CompilerParams(vmem_limit_bytes=VMEM_LIMIT)
    part = jax.ShapeDtypeStruct((groups * total_j * tiles * owned, LANES), F32)
    chunks = tile_chunks(tiles)
    table_rows = levels * grid_count * SUB
    six = jnp.transpose(sixj, (0, 2, 3, 1)).reshape(-1, degrees)
    products = [jax.ShapeDtypeStruct((count, grid_count * channels, LANES), F32) for _, count in chunks]
    first = pl.pallas_call(
        functools.partial(first_body, dims, geometry),
        in_specs=[smem, smem, vmem, vmem, hbm, hbm],
        out_specs=[vmem] * (2 + len(chunks)),
        out_shape=[part, jax.ShapeDtypeStruct((table_rows, columns), F32), *products],
        scratch_shapes=[
            pltpu.VMEM((grid_count, channels, radial), BF16),
            pltpu.VMEM(ps_form.shape, BF16),
            pltpu.VMEM((levels, 2 * SUB * total_j, LANES), F32),
            pltpu.VMEM((degrees * grid_count, LANES), F32),
            pltpu.VMEM((table_rows, 2 * LANES), BF16),
            pltpu.SemaphoreType.DMA((grid_count // BLOCK,)),
            pltpu.SemaphoreType.DMA(()),
        ],
        compiler_params=params,
        name="first_half",
    )
    send, table, *products = first(
        l_atom, kgrid, l_ps.reshape(1, -1), six, amplitude.reshape(grid_count, channels, radial), ps_form
    )
    other = lax.ppermute(send, "core", [(0, 1), (1, 0)])
    keep = pl.pallas_call(
        functools.partial(second_body, geometry),
        in_specs=[smem] + [vmem] * (1 + len(chunks)),
        out_specs=vmem,
        out_shape=part,
        compiler_params=params,
        name="second_half",
    )(l_atom, table, *products)
    mine = (keep + other).reshape(groups * total_j, tiles * owned, 1, LANES)
    got = lax.all_to_all(mine, ("zl", "x", "zh", "y"), split_axis=0, concat_axis=0, tiled=True)
    total = pl.pallas_call(
        functools.partial(sum_body, owned, tiles, groups, total_j),
        in_specs=[vmem],
        out_specs=vmem,
        out_shape=jax.ShapeDtypeStruct((owned, total_j, columns), F32),
        compiler_params=params,
        name="sum_sources",
    )(got.reshape(part.shape))
    return total[:, None]


def solution(mesh):
    fine = Mesh(mesh.devices.reshape(2, 4, 2, 2, 4), ("zl", "x", "core", "zh", "y"))
    ang, slab = ("zl", "x", "core"), ("zh", "y")
    in_specs = (P(ang, None, slab, None), P(), P(), P(), P(), P())
    out_specs = P(ang, slab, None, None)
    return jax.shard_map(local, mesh=fine, in_specs=in_specs, out_specs=out_specs, check_vma=False)
```

time: 69.9 us -> 71.9 us (1.029)
  Pallas kernels: 22.4 us -> 34.3 us
  waiting for transfers between devices: 3.99 us -> 0.01 us
  local copies, waits for them, and re-layouts: 2.9 us -> 0 us
  blocking collectives: 37.4 us -> 35.5 us
  other arithmetic: 2.49 us -> 1.58 us
    pallas_call x1 -> x3, Pallas kernels: 22.4 us -> 34.3 us  [the longest x1 22.8 us: local(): first(l_atom, kgrid, l_ps.reshape(1, -1), six, amplitude.reshape(grid_cou...]
    ppermute x1, waiting for transfers between devices: 3.99 us -> 0.01 us  [local(): other = lax.ppermute(send, 'core', [(0, 1), (1, 0)])]
    unnamed x1 -> x0, local copies, waits for them, and re-layouts: 2.17 us -> none
    all_to_all x1, blocking collectives: 37.4 us -> 35.5 us  [local(): lax.all_to_all(mine, ('zl', 'x', 'zh', 'y'), split_axis=0, concat_axis=0,...]
    transpose x2 -> x0, local copies, waits for them, and re-layouts: 0.73 us -> none  [local(): jnp.transpose(total[:, :, :owned], (2, 0, 1, 3))]
  transfers between devices with their start and end apart: 1 -> 1, of which waited for: 1 -> 0; matrix products, arithmetic and copies ran while one was open for 0% -> 0% of each run, Pallas kernels for 0% -> 13%
where the time goes in v2:
time: 71.9 us; the launch traced here: 71.5 us
  blocking collectives  35.5 us (49%)
  Pallas kernels  34.3 us (48%)
  other arithmetic  1.58 us (2%)
    all_to_all x1, blocking collectives, local(): lax.all_to_all(mine, ('zl', 'x', 'zh', 'y'), split_axis=0, concat_axis=0,...  35.5 us
    pallas_call x1, Pallas kernels, local(): first(l_atom, kgrid, l_ps.reshape(1, -1), six, amplitude.reshape(grid_cou...  22.8 us
    pallas_call x1, Pallas kernels, local(): pl.pallas_call(functools.partial(second_body, geometry), in_specs=[smem]...  9.3 us
    pallas_call x1, Pallas kernels, local(): pl.pallas_call(functools.partial(sum_body, owned, tiles, groups, total_j)...  2.18 us
    add x1, other arithmetic, local(): mine = (keep + other).reshape(groups * total_j, tiles * owned, 1, LANES)  1.58 us
  transfers between devices with their start and end apart: 1, of which 0 were waited for; matrix products, arithmetic and copies ran while one was open for 0% of the time, Pallas kernels for 13%

profile of v2, /device:TPU:0, one launch (start us, length us, event | category | flops | bytes accessed | tf_op | source)
XLA Modules:
  0.0 71.5 jit_solution(4417235695134004293)
XLA Ops:
  0.0 22.8 %first_half.1 = (f32[3136,128]{1,0:T(8,128)}, f32[1024,896]{1,0:T(8,128)}, f32[2,1792,128]{2,1,0:T(8,128)}, f32[2,1792,128]{2,1,0:T(8,128)}, f32[2,1792,128]{2,1,0:T(8,128)}, /*index=5*/f32[1,1792,128]{2,1,0:T(8,128)}) custom-call(s32[112]{0:T(128)} %l_atom.3, f32[8]{0:T(128)} %kgrid.1, s32[1,112]{1,0:T(1,128)} %bitcast.14, f32[512,12]{1,0:T(8,128)} %bitcast.13, ...), custom_call_target="tpu_custom_call" | custom-call | tf_op jit(solution)/shard_map/first_half/pallas_call | solution.py:222
  22.8 0.1 collective-permute-start
  22.9 9.3 %second_half.1 = f32[3136,128]{1,0:T(8,128)} custom-call(s32[112]{0:T(128)} %l_atom.3, f32[1024,896]{1,0:T(8,128)} %get-tuple-element.11.w_ref, f32[2,1792,128]{2,1,0:T(8,128)} %get-tuple-element.12.rest_0_, f32[2,1792,128]{2,1,0:T(8,128)} %get-tuple-element.13.rest_1_, f32[2,1792,128]{2,1,0:T(8,128)} %get-tuple-element.14.rest_2_, ...), custom_call_target="tpu_custom_call" | custom-call | tf_op jit(solution)/shard_map/second_half/pallas_call | solution.py:226
  32.2 0.0 collective-permute-done
  32.2 1.6 %add.3 = f32[3136,128]{1,0:T(8,128)S(1)} add(f32[3136,128]{1,0:T(8,128)} %second_half.1, f32[3136,128]{1,0:T(8,128)S(1)} %collective-permute-done) | non-fusion elementwise | flops 401408 | bytes 4816896 | tf_op jit(solution)/shard_map/add | solution.py:234
  33.8 35.5 %all_to_all.5 = f32[64,49,1,128]{3,2,1,0:T(1,128)} all-to-all(f32[64,49,1,128]{3,2,1,0:T(1,128)S(1)} %bitcast.11), channel_id=1, replica_groups=mesh['zl'=2,'x'=4,'core'=2,'zh'=2,'y'=4] {'zl','x','zh','y'}, dimensions={0} | all-to-all | bytes 3211264 | tf_op jit(solution)/shard_map/all_to_all | solution.py:235
  69.3 2.2 %sum_sources.1 = f32[7,8,896]{2,1,0:T(8,128)} custom-call(f32[3136,128]{1,0:T(8,128)} %bitcast.12), custom_call_target="tpu_custom_call" | custom-call | tf_op jit(solution)/shard_map/sum_sources/pallas_call | solution.py:236
Async XLA Ops:
  22.8 9.4 %collective-permute-start = (f32[3136,128]{1,0:T(8,128)}, f32[3136,128]{1,0:T(8,128)S(1)}, u32[]{:S(2)}, u32[]{:S(2)}) collective-permute-start(f32[3136,128]{1,0:T(8,128)} %get-tuple-element.16), channel_id=1, source_target_pairs={{0,8},{8,0},{1,9},{9,1},{2,10},{10,2},{3,11},{11,3},{4,12},{12,4},... | collective-permute-start | bytes 4816904 | tf_op jit(solution)/shard_map/ppermute | solution.py:225

commit v3 on v2

--- a/solution.py
+++ b/solution.py
@@ -12,9 +12,9 @@
 BF16 = jnp.bfloat16
 LANES = 128
 SUB = 8
-CHUNK = 2
-BLOCK = 4
-VMEM_LIMIT = 56 * 1024 * 1024
+CHUNK = 7
+BLOCK = 8
+VMEM_LIMIT = 28 * 1024 * 1024
 
 
 def iota(shape, axis):
@@ -106,12 +106,12 @@
     return [(t, min(CHUNK, tiles - t)) for t in range(0, tiles, CHUNK)]
 
 
-def first_body(dims, geometry, l_atom, kgrid, lps_ref, six_ref, a_hbm, ps_hbm, *rest):
+def first_body(dims, geometry, la_hbm, kg_hbm, lps_hbm, six_hbm, a_hbm, ps_hbm, *rest):
     grid_count, channels, owned, groups, tiles = geometry
     chunks = tile_chunks(tiles)
     send_ref, w_ref = rest[:2]
     i_refs = rest[2:2 + len(chunks)]
-    a_ref, ps_ref, r1_ref, pq_ref, x3_ref, a_sems, ps_sem = rest[2 + len(chunks):]
+    l_atom, kgrid, lps_ref, six_ref, a_ref, ps_ref, r1_ref, pq_ref, x3_ref, sems, a_sems = rest[2 + len(chunks):]
     core = lax.axis_index("core")
     ang = (lax.axis_index("zl") * lax.axis_size("x") + lax.axis_index("x")) * lax.axis_size("core") + core
     slab = lax.axis_index("zh") * lax.axis_size("y") + lax.axis_index("y")
@@ -120,13 +120,18 @@
         block = pl.ds(m * BLOCK, BLOCK)
         return pltpu.make_async_copy(a_hbm.at[block], a_ref.at[block], a_sems.at[m])
 
-    copy_ps = pltpu.make_async_copy(ps_hbm, ps_ref, ps_sem)
-    copy_ps.start()
+    pairs = ((kg_hbm, kgrid), (six_hbm, six_ref), (lps_hbm, lps_ref), (la_hbm, l_atom), (ps_hbm, ps_ref))
+    small = [pltpu.make_async_copy(source, target, sems.at[i]) for i, (source, target) in enumerate(pairs)]
+    for copy in small:
+        copy.start()
     steps = grid_count // BLOCK
     for m in range(steps):
         copy_a(m).start()
+    for copy in small[:3]:
+        copy.wait()
     build_tables(dims, (ang, slab), kgrid, lps_ref, six_ref, r1_ref, pq_ref, x3_ref, w_ref)
-    copy_ps.wait()
+    for copy in small[3:]:
+        copy.wait()
     rows = BLOCK * channels
     radial = a_ref.shape[-1]
     per_step = groups // steps
@@ -195,32 +200,41 @@
     geometry = (grid_count, channels, owned, groups, tiles)
     smem = pl.BlockSpec(memory_space=pltpu.SMEM)
     vmem = pl.BlockSpec(memory_space=pltpu.VMEM)
-    hbm = pl.BlockSpec(memory_space=pl.ANY)
+    hbm = pl.BlockSpec(memory_space=pltpu.HBM)
     params = pltpu.CompilerParams(vmem_limit_bytes=VMEM_LIMIT)
-    part = jax.ShapeDtypeStruct((groups * total_j * tiles * owned, LANES), F32)
+    part = pltpu.VMEM((groups * total_j * tiles * owned, LANES), F32)
     chunks = tile_chunks(tiles)
     table_rows = levels * grid_count * SUB
     six = jnp.transpose(sixj, (0, 2, 3, 1)).reshape(-1, degrees)
-    products = [jax.ShapeDtypeStruct((count, grid_count * channels, LANES), F32) for _, count in chunks]
+    products = [pltpu.VMEM((count, grid_count * channels, LANES), F32) for _, count in chunks]
     first = pl.pallas_call(
         functools.partial(first_body, dims, geometry),
-        in_specs=[smem, smem, vmem, vmem, hbm, hbm],
+        in_specs=[hbm] * 6,
         out_specs=[vmem] * (2 + len(chunks)),
-        out_shape=[part, jax.ShapeDtypeStruct((table_rows, columns), F32), *products],
+        out_shape=[part, pltpu.VMEM((table_rows, columns), F32), *products],
         scratch_shapes=[
+            pltpu.SMEM(l_atom.shape, jnp.int32),
+            pltpu.SMEM(kgrid.shape, F32),
+            pltpu.VMEM((1, ps_channels), jnp.int32),
+            pltpu.VMEM(six.shape, F32),
             pltpu.VMEM((grid_count, channels, radial), BF16),
             pltpu.VMEM(ps_form.shape, BF16),
             pltpu.VMEM((levels, 2 * SUB * total_j, LANES), F32),
             pltpu.VMEM((degrees * grid_count, LANES), F32),
             pltpu.VMEM((table_rows, 2 * LANES), BF16),
+            pltpu.SemaphoreType.DMA((5,)),
             pltpu.SemaphoreType.DMA((grid_count // BLOCK,)),
-            pltpu.SemaphoreType.DMA(()),
         ],
         compiler_params=params,
         name="first_half",
     )
     send, table, *products = first(
-        l_atom, kgrid, l_ps.reshape(1, -1), six, amplitude.reshape(grid_count, channels, radial), ps_form
+        *(
+            pltpu.with_memory_space_constraint(x, pltpu.HBM)
+            for x in (
+                l_atom, kgrid, l_ps.reshape(1, -1), six, amplitude.reshape(grid_count, channels, radial), ps_form
+            )
+        )
     )
     other = lax.ppermute(send, "core", [(0, 1), (1, 0)])
     keep = pl.pallas_call(

time: 71.9 us -> 55.6 us (0.77)
  Pallas kernels: 34.3 us -> 19.5 us
  other arithmetic: 1.58 us -> 0.16 us
    pallas_call x1, Pallas kernels: 22.8 us -> 14.7 us  [local(): first(*(pltpu.with_memory_space_constraint(x, pltpu.HBM) for x in (l_atom...]
    pallas_call x1, Pallas kernels: 9.3 us -> 4.05 us  [local(): pl.pallas_call(functools.partial(second_body, geometry), in_specs=[smem]...]
    pallas_call x1, Pallas kernels: 2.18 us -> 0.76 us  [local(): pl.pallas_call(functools.partial(sum_body, owned, tiles, groups, total_j)...]
    add x1, other arithmetic: 1.58 us -> 0.16 us  [local(): mine = (keep + other).reshape(groups * total_j, tiles * owned, 1, LANES)]
  transfers between devices with their start and end apart: 1 -> 1, of which waited for: 0 -> 0; matrix products, arithmetic and copies ran while one was open for 0% -> 0% of each run, Pallas kernels for 13% -> 7%
where the time goes in v3:
time: 55.6 us; the launch traced here: 55.2 us
  blocking collectives  35.4 us (64%)
  Pallas kernels  19.5 us (35%)
    all_to_all x1, blocking collectives, local(): lax.all_to_all(mine, ('zl', 'x', 'zh', 'y'), split_axis=0, concat_axis=0,...  35.4 us
    pallas_call x1, Pallas kernels, local(): first(*(pltpu.with_memory_space_constraint(x, pltpu.HBM) for x in (l_atom...  14.7 us
    pallas_call x1, Pallas kernels, local(): pl.pallas_call(functools.partial(second_body, geometry), in_specs=[smem]...  4.05 us
  transfers between devices with their start and end apart: 1, of which 0 were waited for; matrix products, arithmetic and copies ran while one was open for 0% of the time, Pallas kernels for 7%

profile of v3, /device:TPU:0, one launch (start us, length us, event | category | flops | bytes accessed | tf_op | source)
XLA Modules:
  0.0 55.2 jit_solution(12689957618450173757)
XLA Ops:
  0.0 0.0 copy-start
  0.0 14.7 %first_half.1 = (f32[3136,128]{1,0:T(8,128)S(1)}, f32[1024,896]{1,0:T(8,128)S(1)}, f32[7,1792,128]{2,1,0:T(8,128)S(1)}) custom-call(s32[112]{0:T(128)} %l_atom.1, f32[8]{0:T(128)} %kg_hbm.1, s32[1,112]{1,0:T(1,128)} %bitcast.14, f32[512,12]{1,0:T(8,128)} %bitcast.13, bf16[16,112,2048]{2,1,0:T(8,128)(2,1)} %bitcast.11, bf16[2048,896]{1,0:T(8,128)(2,1)} %ps_hbm.1), custom_call_target="tpu_custom_call" | custom-call | tf_op jit(solution)/shard_map/first_half/pallas_call | solution.py:231
  14.7 0.1 collective-permute-start
  14.8 0.0 copy-done
  14.8 4.1 %second_half.1 = f32[3136,128]{1,0:T(8,128)S(1)} custom-call(s32[112]{0:T(128)S(1)} %copy-done, f32[1024,896]{1,0:T(8,128)S(1)} %get-tuple-element.8.w_ref, f32[7,1792,128]{2,1,0:T(8,128)S(1)} %get-tuple-element.9.rest_0_), custom_call_target="tpu_custom_call" | custom-call | tf_op jit(solution)/shard_map/second_half/pallas_call | solution.py:240
  18.9 0.0 collective-permute-done
  18.9 0.2 add.3
  19.1 35.4 %all_to_all.5 = f32[64,49,1,128]{3,2,1,0:T(1,128)S(1)} all-to-all(f32[64,49,1,128]{3,2,1,0:T(1,128)S(1)} %bitcast.12), channel_id=1, replica_groups=mesh['zl'=2,'x'=4,'core'=2,'zh'=2,'y'=4] {'zl','x','zh','y'}, dimensions={0} | all-to-all | bytes 3211264 | tf_op jit(solution)/shard_map/all_to_all | solution.py:249
  54.4 0.8 %sum_sources.1 = f32[7,8,896]{2,1,0:T(8,128)} custom-call(f32[3136,128]{1,0:T(8,128)S(1)} %bitcast.10), custom_call_target="tpu_custom_call" | custom-call | tf_op jit(solution)/shard_map/sum_sources/pallas_call | solution.py:250
Async XLA Ops:
  0.0 14.8 %copy-start = (s32[112]{0:T(128)S(1)}, s32[112]{0:T(128)}, u32[]{:S(2)}) copy-start(s32[112]{0:T(128)} %l_atom.1) | copy-start | bytes 1348
  14.7 4.2 %collective-permute-start = (f32[3136,128]{1,0:T(8,128)S(1)}, f32[3136,128]{1,0:T(8,128)S(1)}, u32[]{:S(2)}, u32[]{:S(2)}) collective-permute-start(f32[3136,128]{1,0:T(8,128)S(1)} %get-tuple-element.10), channel_id=1, source_target_pairs={{0,8},{8,0},{1,9},{9,1},{2,10},{10,2},{3,11},{11,3},{4,12},{12,4},... | collective-permute-start | bytes 4816904 | tf_op jit(solution)/shard_map/ppermute | solution.py:239

commit v4 on v3

v4 whole, which is shorter than its diff:
```python
import functools
import math

import jax
import jax.numpy as jnp
from jax import lax
from jax.experimental import pallas as pl
from jax.experimental.pallas import tpu as pltpu
from jax.sharding import Mesh, PartitionSpec as P

F32 = jnp.float32
BF16 = jnp.bfloat16
LANES = 128
SUB = 8
FIRST = 4
BLOCK = 8
VMEM_LIMIT = 28 * 1024 * 1024


def iota(shape, axis):
    return lax.broadcasted_iota(jnp.int32, shape, axis)


def build_tables(dims, place, kgrid, lps_ref, six_ref, r1_ref, pq_ref, x3_ref, w_ref):
    grid_count, total_points, degrees, levels, kpoints, ps_channels, columns = dims
    shape = (grid_count, LANES)
    position = (place[0] * grid_count + iota(shape, 0)).astype(F32)
    theta = math.pi * (position + 0.5) / total_points
    node = jnp.cos(theta)
    weight = (math.pi / total_points) * jnp.sin(theta)
    kidx = iota(shape, 1) % kpoints
    kcol = jnp.zeros(shape, F32)
    for q in range(kpoints):
        kcol = jnp.where(kidx == q, kgrid[q], kcol)
    krow = kgrid[place[1]]
    qinverse = 1.0 / (1.0 + krow * krow + kcol * kcol - 2.0 * node * krow * kcol)
    scale = weight * qinverse
    series = [jnp.ones(shape, F32), node]
    for degree in range(1, degrees - 1):
        series.append(((2 * degree + 1) * node * series[-1] - degree * series[-2]) / (degree + 1))
    for degree in range(degrees):
        pq_ref[pl.ds(degree * grid_count, grid_count), :] = series[degree] * scale
    half = levels * kpoints
    pad = 2 * SUB
    eye = (iota((pad, degrees), 0) == iota((pad, degrees), 1)).astype(F32)
    turned = lax.dot_general(
        eye, six_ref[...], (((1,), (1,)), ((), ())), precision=lax.Precision.HIGHEST, preferred_element_type=F32
    )
    pairs = levels * levels
    turned = jnp.concatenate([turned[:, j * pairs:(j + 1) * pairs] for j in range(SUB)], axis=0)
    spread_shape = (pairs, levels * LANES)
    source = iota(spread_shape, 0)
    target = iota(spread_shape, 1)
    wanted = (target // LANES) * levels + (target % half) // kpoints
    spread = (source == wanted).astype(F32)
    expanded = jnp.dot(turned, spread, precision=lax.Precision.HIGHEST, preferred_element_type=F32)
    for level in range(levels):
        r1_ref[level] = expanded[:, level * LANES:(level + 1) * LANES]
    low = iota((2 * SUB, LANES), 1) < half
    for level in range(levels):
        coef = [r1_ref[level, pl.ds(degree, SUB, stride=pad), :] for degree in range(degrees)]
        for pair in range(grid_count // 2):
            both = []
            for g in (2 * pair, 2 * pair + 1):
                acc = None
                for degree in range(degrees):
                    row = pq_ref[pl.ds(degree * grid_count + g, SUB, stride=0), :]
                    term = coef[degree] * row
                    acc = term if acc is None else acc + term
                both.append(acc)
            value = jnp.concatenate(both, axis=0)
            hi = value.astype(BF16).astype(F32)
            rest = value - hi
            mid = rest.astype(BF16).astype(F32)
            tail = rest - mid
            rows = pl.ds((level * grid_count + 2 * pair) * SUB, 2 * SUB)
            x3_ref[rows, 0:LANES] = jnp.where(low, hi, mid).astype(BF16)
            x3_ref[rows, LANES:2 * LANES] = jnp.where(low, tail, 0.0).astype(BF16)
    rep_shape = (ps_channels, columns)
    rep = (iota(rep_shape, 0) == iota(rep_shape, 1) // kpoints).astype(F32)
    level_of = jnp.dot(lps_ref[...].astype(F32), rep, preferred_element_type=F32)
    code = level_of.astype(jnp.int32) * kpoints + iota((1, columns), 1) % kpoints
    r = iota((2 * LANES, columns), 0)
    pick = ((r % half == code) & (r < 3 * half)).astype(F32).astype(BF16)
    w_ref[...] = jnp.dot(x3_ref[...], pick, preferred_element_type=F32)


def recouple(geometry, l_atom, i_ref, w_ref, out_ref, chunk, core):
    grid_count, channels, owned, groups, tiles = geometry
    first_tile, count = chunk
    rows, jump = (owned, groups * SUB * owned) if first_tile == 0 else (count * owned, owned)

    def group(d, carry):
        for r in range(owned):
            a = (2 * d + core) * owned + r
            base = l_atom[a] * (grid_count * SUB)
            acc = [None] * count
            for g in range(grid_count):
                for t in range(count):
                    lo = (first_tile + t) * LANES
                    coef = w_ref[pl.ds(pl.multiple_of(base + g * SUB, SUB), SUB), lo:lo + LANES]
                    term = coef * i_ref[t, pl.ds(g * channels + a, SUB, stride=0), :]
                    acc[t] = term if acc[t] is None else acc[t] + term
            for t in range(count):
                out_ref[pl.ds(d * (SUB * rows) + t * jump + r, SUB, stride=rows), :] = acc[t]
        return carry

    lax.fori_loop(0, groups, group, 0)


def multiply(geometry, a_ref, ps_ref, i_ref, chunk, before):
    grid_count, channels = geometry[:2]
    first_tile, count = chunk
    rows = BLOCK * channels

    def step(m, carry):
        before(m)
        left = a_ref[pl.ds(m * BLOCK, BLOCK)].reshape(rows, a_ref.shape[-1])
        right = ps_ref[:, first_tile * LANES:(first_tile + count) * LANES]
        product = jnp.dot(left, right, preferred_element_type=F32)
        for t in range(count):
            i_ref[t, pl.ds(pl.multiple_of(m * rows, rows), rows), :] = product[:, t * LANES:(t + 1) * LANES]
        return carry

    lax.fori_loop(0, grid_count // BLOCK, step, 0)


def first_body(dims, geometry, chunks, la_hbm, kg_hbm, lps_hbm, six_hbm, a_hbm, ps_hbm,
               send_ref, w_ref, i_ref, a_ref, ps_ref,
               l_atom, kgrid, lps_ref, six_ref, r1_ref, pq_ref, x3_ref, sems, a_sems):
    grid_count = geometry[0]
    core = lax.axis_index("core")
    ang = (lax.axis_index("zl") * lax.axis_size("x") + lax.axis_index("x")) * lax.axis_size("core") + core
    slab = lax.axis_index("zh") * lax.axis_size("y") + lax.axis_index("y")

    def copy_a(m):
        block = pl.ds(m * BLOCK, BLOCK)
        return pltpu.make_async_copy(a_hbm.at[block], a_ref.at[block], a_sems.at[m])

    columns = [pl.ds(tile * LANES, count * LANES) for tile, count in chunks]
    pairs = (
        (kg_hbm, kgrid), (six_hbm, six_ref), (lps_hbm, lps_ref), (la_hbm, l_atom),
        (ps_hbm.at[:, columns[0]], ps_ref.at[:, columns[0]]),
        (ps_hbm.at[:, columns[1]], ps_ref.at[:, columns[1]]),
    )
    copies = [pltpu.make_async_copy(source, target, sems.at[i]) for i, (source, target) in enumerate(pairs)]
    for copy in copies[:5]:
        copy.start()
    for m in range(grid_count // BLOCK):
        copy_a(m).start()
    copies[5].start()
    for copy in copies[:3]:
        copy.wait()
    build_tables(dims, (ang, slab), kgrid, lps_ref, six_ref, r1_ref, pq_ref, x3_ref, w_ref)
    for copy in copies[3:5]:
        copy.wait()
    multiply(geometry, a_ref, ps_ref, i_ref, chunks[0], lambda m: copy_a(m).wait())
    recouple(geometry, l_atom, i_ref, w_ref, send_ref, chunks[0], 1 - core)
    copies[5].wait()


def next_body(geometry, chunk, l_atom, w_ref, a_ref, ps_ref, gate, send_ref, keep_ref, i_ref):
    multiply(geometry, a_ref, ps_ref, i_ref, chunk, lambda m: None)
    core = lax.axis_index("core")
    recouple(geometry, l_atom, i_ref, w_ref, send_ref, chunk, 1 - core)
    recouple(geometry, l_atom, i_ref, w_ref, keep_ref, chunk, core)


def own_body(geometry, chunk, l_atom, w_ref, i_ref, keep_ref):
    recouple(geometry, l_atom, i_ref, w_ref, keep_ref, chunk, lax.axis_index("core"))


def split_body(rows, keep_ref, other_ref, z_keep_ref, z_send_ref, x_keep_ref, x_send_ref):
    z = lax.axis_index("zl")
    x = lax.axis_index("x") % 2
    for tile, out_ref in ((z, z_keep_ref), (1 - z, z_send_ref), (2 + x, x_keep_ref), (3 - x, x_send_ref)):
        at = pl.ds(pl.multiple_of(tile * rows, SUB), rows)
        out_ref[...] = keep_ref[at, :] + other_ref[at, :]


def join_body(owned, places, count, zk_ref, zo_ref, xk_ref, xo_ref, keep_ref, other_ref, out_ref,
              z_ref, x_ref, c_ref):
    z_ref[...] = zk_ref[...] + zo_ref[...]
    x_ref[...] = xk_ref[...] + xo_ref[...]
    c_ref[...] = keep_ref[...] + other_ref[...]
    rows = (count + 2) * owned

    def group(d, carry):
        for n, (ref, width) in enumerate(((z_ref, owned), (x_ref, owned), (c_ref, count * owned))):
            for r in range(width):
                part = ref[pl.ds(d * (SUB * width) + r, SUB, stride=width), :]
                out_ref[pl.ds(d * (SUB * rows) + n * owned + r, SUB, stride=rows), :] = part
        return carry

    lax.fori_loop(0, places // SUB, group, 0)


def sum_body(owned, sources, total_j, chunks, got_ref, out_ref):
    first, count = chunks[0][1], chunks[1][1]
    rows = (count + 2) * owned
    everyone = list(range(sources))
    half = sources // 2
    held = {0: (0, everyone[:half]), 1: (0, everyone[half:]), 2: (1, everyone[0::2]), 3: (1, everyone[1::2])}
    for t in range(count):
        held[first + t] = (2 + t, everyone)
    for r in range(owned):
        for t, (block, members) in held.items():
            acc = None
            for s in members:
                part = got_ref[pl.ds(s * total_j * rows + block * owned + r, total_j, stride=rows), :]
                acc = part if acc is None else acc + part
            out_ref[r, :, t * LANES:(t + 1) * LANES] = acc


def local(amplitude, ps_form, kgrid, l_atom, l_ps, sixj):
    grid_count, channels, slab_points, radial = amplitude.shape
    columns = ps_form.shape[1]
    kpoints = kgrid.shape[0]
    total_j, degrees, levels, _ = sixj.shape
    ps_channels = l_ps.shape[0]
    ang_size = lax.axis_size(("zl", "x", "core"))
    owned = channels // ang_size
    groups = ang_size // 2
    tiles = columns // LANES
    chunks = ((0, FIRST), (FIRST, tiles - FIRST))
    dims = (grid_count, grid_count * ang_size, degrees, levels, kpoints, ps_channels, columns)
    geometry = (grid_count, channels, owned, groups, tiles)
    smem = pl.BlockSpec(memory_space=pltpu.SMEM)
    vmem = pl.BlockSpec(memory_space=pltpu.VMEM)
    hbm = pl.BlockSpec(memory_space=pltpu.HBM)
    params = pltpu.CompilerParams(vmem_limit_bytes=VMEM_LIMIT)
    parts = [pltpu.VMEM((groups * total_j * count * owned, LANES), F32) for _, count in chunks]
    products = [pltpu.VMEM((count, grid_count * channels, LANES), F32) for _, count in chunks]
    table_rows = levels * grid_count * SUB
    six = jnp.transpose(sixj, (0, 2, 3, 1)).reshape(-1, degrees)
    inputs = (l_atom, kgrid, l_ps.reshape(1, -1), six, amplitude.reshape(grid_count, channels, radial), ps_form)
    send, table, product, left, right = pl.pallas_call(
        functools.partial(first_body, dims, geometry, chunks),
        in_specs=[hbm] * 6,
        out_specs=[vmem] * 5,
        out_shape=[
            parts[0],
            pltpu.VMEM((table_rows, columns), F32),
            products[0],
            pltpu.VMEM((grid_count, channels, radial), BF16),
            pltpu.VMEM(ps_form.shape, BF16),
        ],
        scratch_shapes=[
            pltpu.SMEM(l_atom.shape, jnp.int32),
            pltpu.SMEM(kgrid.shape, F32),
            pltpu.VMEM((1, ps_channels), jnp.int32),
            pltpu.VMEM(six.shape, F32),
            pltpu.VMEM((levels, 2 * SUB * total_j, LANES), F32),
            pltpu.VMEM((degrees * grid_count, LANES), F32),
            pltpu.VMEM((table_rows, 2 * LANES), BF16),
            pltpu.SemaphoreType.DMA((6,)),
            pltpu.SemaphoreType.DMA((grid_count // BLOCK,)),
        ],
        compiler_params=params,
        name="first_chunk",
    )(*(pltpu.with_memory_space_constraint(x, pltpu.HBM) for x in inputs))
    def own_part(n, product):
        return pl.pallas_call(
            functools.partial(own_body, geometry, chunks[n]),
            in_specs=[smem, vmem, vmem],
            out_specs=vmem,
            out_shape=parts[n],
            compiler_params=params,
            name="own_part",
        )(l_atom, table, product)

    places = groups * total_j
    swap = [(0, 1), (1, 0)]
    other = lax.ppermute(send, "core", swap)
    tile_part = pltpu.VMEM((places * owned, LANES), F32)
    z_keep, z_send, x_keep, x_send = pl.pallas_call(
        functools.partial(split_body, places * owned),
        in_specs=[vmem] * 2,
        out_specs=[vmem] * 4,
        out_shape=[tile_part] * 4,
        compiler_params=params,
        name="split_tiles",
    )(own_part(0, product), other)
    z_other = lax.ppermute(z_send, "zl", swap)
    x_other = lax.ppermute(x_send, "x", [(0, 1), (1, 0), (2, 3), (3, 2)])
    send, keep = pl.pallas_call(
        functools.partial(next_body, geometry, chunks[1]),
        in_specs=[smem, vmem, vmem, vmem, pl.BlockSpec(memory_space=pl.ANY)],
        out_specs=[vmem] * 2,
        out_shape=[parts[1]] * 2,
        scratch_shapes=[products[1]],
        compiler_params=params,
        name="next_chunk",
    )(l_atom, table, left, right, z_keep)
    send, z_other, x_other = lax.optimization_barrier((send, z_other, x_other))
    other = lax.ppermute(send, "core", swap)
    count = chunks[1][1]
    rows = (count + 2) * owned
    joined = pl.pallas_call(
        functools.partial(join_body, owned, places, count),
        in_specs=[vmem] * 6,
        out_specs=vmem,
        out_shape=pltpu.VMEM((places * rows, LANES), F32),
        scratch_shapes=[pltpu.VMEM((places * n * owned, LANES), F32) for n in (1, 1, count)],
        compiler_params=params,
        name="join_rows",
    )(z_keep, z_other, x_keep, x_other, keep, other)
    tile = joined.reshape(places, rows, 1, LANES)
    got = lax.all_to_all(tile, ("zl", "x", "zh", "y"), split_axis=0, concat_axis=0, tiled=True)
    total = pl.pallas_call(
        functools.partial(sum_body, owned, groups, total_j, chunks),
        in_specs=[vmem],
        out_specs=vmem,
        out_shape=jax.ShapeDtypeStruct((owned, total_j, columns), F32),
        compiler_params=params,
        name="sum_sources",
    )(got.reshape(-1, LANES))
    return total[:, None]


def solution(mesh):
    fine = Mesh(mesh.devices.reshape(2, 4, 2, 2, 4), ("zl", "x", "core", "zh", "y"))
    ang, slab = ("zl", "x", "core"), ("zh", "y")
    in_specs = (P(ang, None, slab, None), P(), P(), P(), P(), P())
    out_specs = P(ang, slab, None, None)
    return jax.shard_map(local, mesh=fine, in_specs=in_specs, out_specs=out_specs, check_vma=False)
```

time: 55.6 us -> 56.6 us (1.018)
  blocking collectives: 35.4 us -> 30 us
  starting transfers between devices: 0.09 us -> 3.73 us
  waiting for transfers between devices: 0.01 us -> 2.14 us
  Pallas kernels: 19.5 us -> 20.5 us
    all_to_all x1, blocking collectives: 35.4 us -> 30 us  [local(): lax.all_to_all(tile, ('zl', 'x', 'zh', 'y'), split_axis=0, concat_axis=0,...]
    ppermute x1 -> x4, starting transfers between devices: 0.09 us -> 3.73 us  [the longest x1 2.08 us: local(): z_other = lax.ppermute(z_send, 'zl', swap)]
    ppermute x1 -> x4, waiting for transfers between devices: 0.01 us -> 2.14 us  [the longest x2 2.13 us: local(): other = lax.ppermute(send, 'core', swap)]
    pallas_call x3 -> x6, Pallas kernels: 19.5 us -> 20.5 us  [the longest x1 9.14 us: local(): pl.pallas_call(functools.partial(first_body, dims, geometry, chunks), in_...]
  transfers between devices with their start and end apart: 1 -> 4, of which waited for: 0 -> 1; matrix products, arithmetic and copies ran while one was open for 0% -> 0% of each run, Pallas kernels for 7% -> 18%
where the time goes in v4:
time: 56.6 us; the launch traced here: 56.5 us
  blocking collectives  30 us (53%)
  Pallas kernels  20.5 us (36%)
  starting transfers between devices  3.73 us (7%)
  waiting for transfers between devices  2.14 us (4%)
    all_to_all x1, blocking collectives, local(): lax.all_to_all(tile, ('zl', 'x', 'zh', 'y'), split_axis=0, concat_axis=0,...  30 us
    pallas_call x1, Pallas kernels, local(): pl.pallas_call(functools.partial(first_body, dims, geometry, chunks), in_...  9.14 us
    pallas_call x1, Pallas kernels, local(): pl.pallas_call(functools.partial(next_body, geometry, chunks[1]), in_spec...  7.74 us
    pallas_call x1, Pallas kernels, own_part(): pl.pallas_call(functools.partial(own_body, geometry, chunks[n]), in_specs...  2.55 us
    ppermute x2, waiting for transfers between devices, local(): other = lax.ppermute(send, 'core', swap)  2.13 us
    ppermute x1, starting transfers between devices, local(): z_other = lax.ppermute(z_send, 'zl', swap)  2.08 us
    ppermute x1, starting transfers between devices, local(): x_other = lax.ppermute(x_send, 'x', [(0, 1), (1, 0), (2, 3), (3, 2)])  1.48 us
  transfers between devices with their start and end apart: 4, of which 1 were waited for; matrix products, arithmetic and copies ran while one was open for 0% of the time, Pallas kernels for 18%

profile of v4, /device:TPU:0, one launch (start us, length us, event | category | flops | bytes accessed | tf_op | source)
XLA Modules:
  0.0 56.5 jit_solution(7843087708376339212)
XLA Ops:
  0.0 0.0 copy-start
  0.0 9.1 %first_chunk.1 = (f32[1792,128]{1,0:T(8,128)S(1)}, f32[1024,896]{1,0:T(8,128)S(1)}, f32[4,1792,128]{2,1,0:T(8,128)S(1)}, bf16[16,112,2048]{2,1,0:T(8,128)(2,1)S(1)}, bf16[2048,896]{1,0:T(8,128)(2,1)S(1)}) custom-call(s32[112]{0:T(128)} %l_atom.3, f32[8]{0:T(128)} %kg_hbm.1, s32[1,112]{1,0:T(1,128)} %bitcast.14, f32[512,12]{1,0:T(8,128)} %bitcast.13, ...), custom_call_target="tpu_custom_call" | custom-call | tf_op jit(solution)/shard_map/first_chunk/pallas_call | solution.py:237
  9.2 0.1 collective-permute-start
  9.2 0.0 copy-done
  9.3 2.5 %own_part.1.keep_ref = f32[1792,128]{1,0:T(8,128)S(1)} custom-call(s32[112]{0:T(128)S(1)} %copy-done, f32[1024,896]{1,0:T(8,128)S(1)} %get-tuple-element.19.w_ref, f32[4,1792,128]{2,1,0:T(8,128)S(1)} %get-tuple-element.20.i_ref), custom_call_target="tpu_custom_call" | custom-call | tf_op jit(solution)/shard_map/own_part/pallas_call | solution.py:263
  11.8 0.0 collective-permute-done.other_ref
  11.8 0.1 split_tiles.1
  11.9 2.1 %collective-permute-start.1 = (f32[448,128]{1,0:T(8,128)S(1)}, f32[448,128]{1,0:T(8,128)S(1)}, u32[]{:S(2)}, u32[]{:S(2)}) collective-permute-start(f32[448,128]{1,0:T(8,128)S(1)} %get-tuple-element.26), channel_id=1, source_target_pairs={{0,64},{64,0},{1,65},{65,1},{2,66},{66,2},{3,67},{67,3},{4,68},{68... | collective-permute-start | bytes 688136 | tf_op jit(solution)/shard_map/ppermute | solution.py:284
  14.0 1.5 %collective-permute-start.2 = (f32[448,128]{1,0:T(8,128)S(1)}, f32[448,128]{1,0:T(8,128)S(1)}, u32[]{:S(2)}, u32[]{:S(2)}) collective-permute-start(f32[448,128]{1,0:T(8,128)S(1)} %get-tuple-element.27), channel_id=1, source_target_pairs={{0,16},{16,0},{32,48},{48,32},{1,17},{17,1},{33,49},{49,33},{2,18}... | collective-permute-start | bytes 688136 | tf_op jit(solution)/shard_map/ppermute | solution.py:285
  15.5 7.7 %next_chunk.1 = (f32[1344,128]{1,0:T(8,128)S(1)}, f32[1344,128]{1,0:T(8,128)S(1)}) custom-call(s32[112]{0:T(128)S(1)} %copy-done, f32[1024,896]{1,0:T(8,128)S(1)} %get-tuple-element.19.w_ref, bf16[16,112,2048]{2,1,0:T(8,128)(2,1)S(1)} %get-tuple-element.23.a_ref, bf16[2048,896]{1,0:T(8,128)(2,1)S(1)} %get-tuple-element.24.ps_ref, ...), custom_call_target="tpu_custom_call" | custom-call | tf_op jit(solution)/shard_map/next_chunk/pallas_call | solution.py:286
  23.2 0.0 collective-permute-done.1.zo_ref
  23.2 0.0 collective-permute-done.2.xo_ref
  23.3 0.1 collective-permute-start.3
  23.3 2.1 %collective-permute-done.3.other_ref = f32[1344,128]{1,0:T(8,128)S(1)} collective-permute-done((f32[1344,128]{1,0:T(8,128)S(1)}, f32[1344,128]{1,0:T(8,128)S(1)}, u32[]{:S(2)}, u32[]{:S(2)}) %collective-permute-start.3) | collective-permute-done | bytes 688160 | tf_op jit(solution)/shard_map/ppermute | solution.py:296
  25.5 0.3 join_rows.1
  25.7 30.0 %all_to_all.5 = f32[64,35,1,128]{3,2,1,0:T(1,128)S(1)} all-to-all(f32[64,35,1,128]{3,2,1,0:T(1,128)S(1)} %bitcast.11), channel_id=1, replica_groups=mesh['zl'=2,'x'=4,'core'=2,'zh'=2,'y'=4] {'zl','x','zh','y'}, dimensions={0} | all-to-all | bytes 2293760 | tf_op jit(solution)/shard_map/all_to_all | solution.py:309
  55.7 0.7 %sum_sources.1 = f32[7,8,896]{2,1,0:T(8,128)} custom-call(f32[2240,128]{1,0:T(8,128)S(1)} %bitcast.10), custom_call_target="tpu_custom_call" | custom-call | tf_op jit(solution)/shard_map/sum_sources/pallas_call | solution.py:310
Async XLA Ops:
  0.0 9.2 %copy-start = (s32[112]{0:T(128)S(1)}, s32[112]{0:T(128)}, u32[]{:S(2)}) copy-start(s32[112]{0:T(128)} %l_atom.3) | copy-start | bytes 1348
  9.2 2.7 %collective-permute-start = (f32[1792,128]{1,0:T(8,128)S(1)}, f32[1792,128]{1,0:T(8,128)S(1)}, u32[]{:S(2)}, u32[]{:S(2)}) collective-permute-start(f32[1792,128]{1,0:T(8,128)S(1)} %get-tuple-element.21), channel_id=1, source_target_pairs={{0,8},{8,0},{1,9},{9,1},{2,10},{10,2},{3,11},{11,3},{4,12},{12,4},... | collective-permute-start | bytes 2752520 | tf_op jit(solution)/shard_map/ppermute | solution.py:274
  11.9 11.3 %collective-permute-start.1 = (f32[448,128]{1,0:T(8,128)S(1)}, f32[448,128]{1,0:T(8,128)S(1)}, u32[]{:S(2)}, u32[]{:S(2)}) collective-permute-start(f32[448,128]{1,0:T(8,128)S(1)} %get-tuple-element.26), channel_id=1, source_target_pairs={{0,64},{64,0},{1,65},{65,1},{2,66},{66,2},{3,67},{67,3},{4,68},{68... | collective-permute-start | bytes 688136 | tf_op jit(solution)/shard_map/ppermute | solution.py:284
  14.0 9.2 %collective-permute-start.2 = (f32[448,128]{1,0:T(8,128)S(1)}, f32[448,128]{1,0:T(8,128)S(1)}, u32[]{:S(2)}, u32[]{:S(2)}) collective-permute-start(f32[448,128]{1,0:T(8,128)S(1)} %get-tuple-element.27), channel_id=1, source_target_pairs={{0,16},{16,0},{32,48},{48,32},{1,17},{17,1},{33,49},{49,33},{2,18}... | collective-permute-start | bytes 688136 | tf_op jit(solution)/shard_map/ppermute | solution.py:285
  23.3 2.2 %collective-permute-start.3 = (f32[1344,128]{1,0:T(8,128)S(1)}, f32[1344,128]{1,0:T(8,128)S(1)}, u32[]{:S(2)}, u32[]{:S(2)}) collective-permute-start(f32[1344,128]{1,0:T(8,128)S(1)} %get-tuple-element.32), channel_id=1, source_target_pairs={{0,8},{8,0},{1,9},{9,1},{2,10},{10,2},{3,11},{11,3},{4,12},{12,4},... | collective-permute-start | bytes 2064392 | tf_op jit(solution)/shard_map/ppermute | solution.py:296

commit v5 on v4

--- a/solution.py
+++ b/solution.py
@@ -159,11 +159,9 @@
     copies[5].wait()
 
 
-def next_body(geometry, chunk, l_atom, w_ref, a_ref, ps_ref, gate, send_ref, keep_ref, i_ref):
+def next_body(geometry, chunk, l_atom, w_ref, a_ref, ps_ref, gate, send_ref, i_ref):
     multiply(geometry, a_ref, ps_ref, i_ref, chunk, lambda m: None)
-    core = lax.axis_index("core")
-    recouple(geometry, l_atom, i_ref, w_ref, send_ref, chunk, 1 - core)
-    recouple(geometry, l_atom, i_ref, w_ref, keep_ref, chunk, core)
+    recouple(geometry, l_atom, i_ref, w_ref, send_ref, chunk, 1 - lax.axis_index("core"))
 
 
 def own_body(geometry, chunk, l_atom, w_ref, i_ref, keep_ref):
@@ -283,17 +281,17 @@
     )(own_part(0, product), other)
     z_other = lax.ppermute(z_send, "zl", swap)
     x_other = lax.ppermute(x_send, "x", [(0, 1), (1, 0), (2, 3), (3, 2)])
-    send, keep = pl.pallas_call(
+    send, product = pl.pallas_call(
         functools.partial(next_body, geometry, chunks[1]),
         in_specs=[smem, vmem, vmem, vmem, pl.BlockSpec(memory_space=pl.ANY)],
         out_specs=[vmem] * 2,
-        out_shape=[parts[1]] * 2,
-        scratch_shapes=[products[1]],
+        out_shape=[parts[1], products[1]],
         compiler_params=params,
         name="next_chunk",
     )(l_atom, table, left, right, z_keep)
-    send, z_other, x_other = lax.optimization_barrier((send, z_other, x_other))
+    send, product, z_other, x_other = lax.optimization_barrier((send, product, z_other, x_other))
     other = lax.ppermute(send, "core", swap)
+    keep = own_part(1, product)
     count = chunks[1][1]
     rows = (count + 2) * owned
     joined = pl.pallas_call(

time: 56.6 us -> 55.4 us (0.979)
  waiting for transfers between devices: 2.14 us -> 0.02 us
  Pallas kernels: 20.5 us -> 21.1 us
    ppermute x2, waiting for transfers between devices: 2.13 us -> 0.01 us  [local(): other = lax.ppermute(send, 'core', swap)]
    pallas_call x1 -> x2, Pallas kernels: 2.55 us -> 4.66 us  [own_part(): pl.pallas_call(functools.partial(own_body, geometry, chunks[n]), in_specs...]
    pallas_call x1, Pallas kernels: 7.74 us -> 6.21 us  [local(): pl.pallas_call(functools.partial(next_body, geometry, chunks[1]), in_spec...]
  transfers between devices with their start and end apart: 4 -> 4, of which waited for: 1 -> 0; matrix products, arithmetic and copies ran while one was open for 0% -> 0% of each run, Pallas kernels for 18% -> 20%
where the time goes in v5:
time: 55.4 us; the launch traced here: 55.3 us
  blocking collectives  30.3 us (55%)
  Pallas kernels  21.1 us (38%)
  starting transfers between devices  3.73 us (7%)
    all_to_all x1, blocking collectives, local(): lax.all_to_all(tile, ('zl', 'x', 'zh', 'y'), split_axis=0, concat_axis=0,...  30.3 us
    pallas_call x1, Pallas kernels, local(): pl.pallas_call(functools.partial(first_body, dims, geometry, chunks), in_...  9.14 us
    pallas_call x1, Pallas kernels, local(): pl.pallas_call(functools.partial(next_body, geometry, chunks[1]), in_spec...  6.21 us
    pallas_call x2, Pallas kernels, own_part(): pl.pallas_call(functools.partial(own_body, geometry, chunks[n]), in_specs...  4.66 us
    ppermute x1, starting transfers between devices, local(): z_other = lax.ppermute(z_send, 'zl', swap)  2.08 us
    ppermute x1, starting transfers between devices, local(): x_other = lax.ppermute(x_send, 'x', [(0, 1), (1, 0), (2, 3), (3, 2)])  1.48 us
  transfers between devices with their start and end apart: 4, of which 0 were waited for; matrix products, arithmetic and copies ran while one was open for 0% of the time, Pallas kernels for 20%

profile of v5, /device:TPU:0, one launch (start us, length us, event | category | flops | bytes accessed | tf_op | source)
XLA Modules:
  0.0 55.3 jit_solution(13352424266348614957)
XLA Ops:
  0.0 0.0 copy-start
  0.0 9.1 %first_chunk.1 = (f32[1792,128]{1,0:T(8,128)S(1)}, f32[1024,896]{1,0:T(8,128)S(1)}, f32[4,1792,128]{2,1,0:T(8,128)S(1)}, bf16[16,112,2048]{2,1,0:T(8,128)(2,1)S(1)}, bf16[2048,896]{1,0:T(8,128)(2,1)S(1)}) custom-call(s32[112]{0:T(128)} %l_atom.5, f32[8]{0:T(128)} %kg_hbm.1, s32[1,112]{1,0:T(1,128)} %bitcast.14, f32[512,12]{1,0:T(8,128)} %bitcast.13, ...), custom_call_target="tpu_custom_call" | custom-call | tf_op jit(solution)/shard_map/first_chunk/pallas_call | solution.py:235
  9.2 0.1 collective-permute-start
  9.2 0.0 copy-done
  9.3 2.5 %own_part.2.keep_ref = f32[1792,128]{1,0:T(8,128)S(1)} custom-call(s32[112]{0:T(128)S(1)} %copy-done, f32[1024,896]{1,0:T(8,128)S(1)} %get-tuple-element.20.w_ref, f32[4,1792,128]{2,1,0:T(8,128)S(1)} %get-tuple-element.21.i_ref), custom_call_target="tpu_custom_call" | custom-call | tf_op jit(solution)/shard_map/own_part/pallas_call | solution.py:261
  11.8 0.0 collective-permute-done.other_ref
  11.8 0.1 split_tiles.1
  11.9 2.1 %collective-permute-start.1 = (f32[448,128]{1,0:T(8,128)S(1)}, f32[448,128]{1,0:T(8,128)S(1)}, u32[]{:S(2)}, u32[]{:S(2)}) collective-permute-start(f32[448,128]{1,0:T(8,128)S(1)} %get-tuple-element.28), channel_id=1, source_target_pairs={{0,64},{64,0},{1,65},{65,1},{2,66},{66,2},{3,67},{67,3},{4,68},{68... | collective-permute-start | bytes 688136 | tf_op jit(solution)/shard_map/ppermute | solution.py:282
  14.0 1.5 %collective-permute-start.2 = (f32[448,128]{1,0:T(8,128)S(1)}, f32[448,128]{1,0:T(8,128)S(1)}, u32[]{:S(2)}, u32[]{:S(2)}) collective-permute-start(f32[448,128]{1,0:T(8,128)S(1)} %get-tuple-element.29), channel_id=1, source_target_pairs={{0,16},{16,0},{32,48},{48,32},{1,17},{17,1},{33,49},{49,33},{2,18}... | collective-permute-start | bytes 688136 | tf_op jit(solution)/shard_map/ppermute | solution.py:283
  15.5 6.2 %next_chunk.1 = (f32[1344,128]{1,0:T(8,128)S(1)}, f32[3,1792,128]{2,1,0:T(8,128)S(1)}) custom-call(s32[112]{0:T(128)S(1)} %copy-done, f32[1024,896]{1,0:T(8,128)S(1)} %get-tuple-element.20.w_ref, bf16[16,112,2048]{2,1,0:T(8,128)(2,1)S(1)} %get-tuple-element.24.a_ref, bf16[2048,896]{1,0:T(8,128)(2,1)S(1)} %get-tuple-element.25.ps_ref, ...), custom_call_target="tpu_custom_call" | custom-call | tf_op jit(solution)/shard_map/next_chunk/pallas_call | solution.py:284
  21.7 0.0 collective-permute-done.1.zo_ref
  21.7 0.0 collective-permute-done.2.xo_ref
  21.7 0.1 collective-permute-start.3
  21.8 2.1 %own_part.3.keep_ref = f32[1344,128]{1,0:T(8,128)S(1)} custom-call(s32[112]{0:T(128)S(1)} %copy-done, f32[1024,896]{1,0:T(8,128)S(1)} %get-tuple-element.20.w_ref, f32[3,1792,128]{2,1,0:T(8,128)S(1)} %get-tuple-element.33.i_ref), custom_call_target="tpu_custom_call" | custom-call | tf_op jit(solution)/shard_map/own_part/pallas_call | solution.py:261
  23.9 0.0 collective-permute-done.3.other_ref
  24.0 0.3 join_rows.1
  24.2 30.3 %all_to_all.5 = f32[64,35,1,128]{3,2,1,0:T(1,128)S(1)} all-to-all(f32[64,35,1,128]{3,2,1,0:T(1,128)S(1)} %bitcast.11), channel_id=1, replica_groups=mesh['zl'=2,'x'=4,'core'=2,'zh'=2,'y'=4] {'zl','x','zh','y'}, dimensions={0} | all-to-all | bytes 2293760 | tf_op jit(solution)/shard_map/all_to_all | solution.py:307
  54.6 0.7 %sum_sources.1 = f32[7,8,896]{2,1,0:T(8,128)} custom-call(f32[2240,128]{1,0:T(8,128)S(1)} %bitcast.10), custom_call_target="tpu_custom_call" | custom-call | tf_op jit(solution)/shard_map/sum_sources/pallas_call | solution.py:308
Async XLA Ops:
  0.0 9.2 %copy-start = (s32[112]{0:T(128)S(1)}, s32[112]{0:T(128)}, u32[]{:S(2)}) copy-start(s32[112]{0:T(128)} %l_atom.5) | copy-start | bytes 1348
  9.2 2.7 %collective-permute-start = (f32[1792,128]{1,0:T(8,128)S(1)}, f32[1792,128]{1,0:T(8,128)S(1)}, u32[]{:S(2)}, u32[]{:S(2)}) collective-permute-start(f32[1792,128]{1,0:T(8,128)S(1)} %get-tuple-element.22), channel_id=1, source_target_pairs={{0,8},{8,0},{1,9},{9,1},{2,10},{10,2},{3,11},{11,3},{4,12},{12,4},... | collective-permute-start | bytes 2752520 | tf_op jit(solution)/shard_map/ppermute | solution.py:272
  11.9 9.8 %collective-permute-start.1 = (f32[448,128]{1,0:T(8,128)S(1)}, f32[448,128]{1,0:T(8,128)S(1)}, u32[]{:S(2)}, u32[]{:S(2)}) collective-permute-start(f32[448,128]{1,0:T(8,128)S(1)} %get-tuple-element.28), channel_id=1, source_target_pairs={{0,64},{64,0},{1,65},{65,1},{2,66},{66,2},{3,67},{67,3},{4,68},{68... | collective-permute-start | bytes 688136 | tf_op jit(solution)/shard_map/ppermute | solution.py:282
  14.0 7.7 %collective-permute-start.2 = (f32[448,128]{1,0:T(8,128)S(1)}, f32[448,128]{1,0:T(8,128)S(1)}, u32[]{:S(2)}, u32[]{:S(2)}) collective-permute-start(f32[448,128]{1,0:T(8,128)S(1)} %get-tuple-element.29), channel_id=1, source_target_pairs={{0,16},{16,0},{32,48},{48,32},{1,17},{17,1},{33,49},{49,33},{2,18}... | collective-permute-start | bytes 688136 | tf_op jit(solution)/shard_map/ppermute | solution.py:283
  21.7 2.2 %collective-permute-start.3 = (f32[1344,128]{1,0:T(8,128)S(1)}, f32[1344,128]{1,0:T(8,128)S(1)}, u32[]{:S(2)}, u32[]{:S(2)}) collective-permute-start(f32[1344,128]{1,0:T(8,128)S(1)} %get-tuple-element.34), channel_id=1, source_target_pairs={{0,8},{8,0},{1,9},{9,1},{2,10},{10,2},{3,11},{11,3},{4,12},{12,4},... | collective-permute-start | bytes 2064392 | tf_op jit(solution)/shard_map/ppermute | solution.py:293

commit v6 on v5

--- a/solution.py
+++ b/solution.py
@@ -12,7 +12,7 @@
 BF16 = jnp.bfloat16
 LANES = 128
 SUB = 8
-FIRST = 4
+FIRST = 6
 BLOCK = 8
 VMEM_LIMIT = 28 * 1024 * 1024
 
@@ -168,23 +168,28 @@
     recouple(geometry, l_atom, i_ref, w_ref, keep_ref, chunk, lax.axis_index("core"))
 
 
-def split_body(rows, keep_ref, other_ref, z_keep_ref, z_send_ref, x_keep_ref, x_send_ref):
+def split_body(rows, keep_ref, other_ref, z_keep_ref, z_send_ref, x_keep_ref, x_send_ref, y_keep_ref, y_send_ref):
     z = lax.axis_index("zl")
     x = lax.axis_index("x") % 2
-    for tile, out_ref in ((z, z_keep_ref), (1 - z, z_send_ref), (2 + x, x_keep_ref), (3 - x, x_send_ref)):
+    y = (lax.axis_index("x") + 1) % 2
+    for tile, out_ref in (
+        (z, z_keep_ref), (1 - z, z_send_ref), (2 + x, x_keep_ref), (3 - x, x_send_ref),
+        (4 + y, y_keep_ref), (5 - y, y_send_ref),
+    ):
         at = pl.ds(pl.multiple_of(tile * rows, SUB), rows)
         out_ref[...] = keep_ref[at, :] + other_ref[at, :]
 
 
-def join_body(owned, places, count, zk_ref, zo_ref, xk_ref, xo_ref, keep_ref, other_ref, out_ref,
-              z_ref, x_ref, c_ref):
+def join_body(owned, places, count, zk_ref, zo_ref, xk_ref, xo_ref, yk_ref, yo_ref, keep_ref, other_ref, out_ref,
+              z_ref, x_ref, y_ref, c_ref):
     z_ref[...] = zk_ref[...] + zo_ref[...]
     x_ref[...] = xk_ref[...] + xo_ref[...]
+    y_ref[...] = yk_ref[...] + yo_ref[...]
     c_ref[...] = keep_ref[...] + other_ref[...]
-    rows = (count + 2) * owned
+    rows = (count + 3) * owned
 
     def group(d, carry):
-        for n, (ref, width) in enumerate(((z_ref, owned), (x_ref, owned), (c_ref, count * owned))):
+        for n, (ref, width) in enumerate(((z_ref, owned), (x_ref, owned), (y_ref, owned), (c_ref, count * owned))):
             for r in range(width):
                 part = ref[pl.ds(d * (SUB * width) + r, SUB, stride=width), :]
                 out_ref[pl.ds(d * (SUB * rows) + n * owned + r, SUB, stride=rows), :] = part
@@ -195,12 +200,13 @@
 
 def sum_body(owned, sources, total_j, chunks, got_ref, out_ref):
     first, count = chunks[0][1], chunks[1][1]
-    rows = (count + 2) * owned
+    rows = (count + 3) * owned
     everyone = list(range(sources))
     half = sources // 2
-    held = {0: (0, everyone[:half]), 1: (0, everyone[half:]), 2: (1, everyone[0::2]), 3: (1, everyone[1::2])}
+    held = {0: (0, everyone[:half]), 1: (0, everyone[half:]), 2: (1, everyone[0::2]), 3: (1, everyone[1::2]),
+            4: (2, everyone[1::2]), 5: (2, everyone[0::2])}
     for t in range(count):
-        held[first + t] = (2 + t, everyone)
+        held[first + t] = (3 + t, everyone)
     for r in range(owned):
         for t, (block, members) in held.items():
             acc = None
@@ -271,16 +277,17 @@
     swap = [(0, 1), (1, 0)]
     other = lax.ppermute(send, "core", swap)
     tile_part = pltpu.VMEM((places * owned, LANES), F32)
-    z_keep, z_send, x_keep, x_send = pl.pallas_call(
+    z_keep, z_send, x_keep, x_send, y_keep, y_send = pl.pallas_call(
         functools.partial(split_body, places * owned),
         in_specs=[vmem] * 2,
-        out_specs=[vmem] * 4,
-        out_shape=[tile_part] * 4,
+        out_specs=[vmem] * 6,
+        out_shape=[tile_part] * 6,
         compiler_params=params,
         name="split_tiles",
     )(own_part(0, product), other)
     z_other = lax.ppermute(z_send, "zl", swap)
     x_other = lax.ppermute(x_send, "x", [(0, 1), (1, 0), (2, 3), (3, 2)])
+    y_other = lax.ppermute(y_send, "x", [(0, 3), (3, 0), (1, 2), (2, 1)])
     send, product = pl.pallas_call(
         functools.partial(next_body, geometry, chunks[1]),
         in_specs=[smem, vmem, vmem, vmem, pl.BlockSpec(memory_space=pl.ANY)],
@@ -289,20 +296,20 @@
         compiler_params=params,
         name="next_chunk",
     )(l_atom, table, left, right, z_keep)
-    send, product, z_other, x_other = lax.optimization_barrier((send, product, z_other, x_other))
+    send, product, z_other, x_other, y_other = lax.optimization_barrier((send, product, z_other, x_other, y_other))
     other = lax.ppermute(send, "core", swap)
     keep = own_part(1, product)
     count = chunks[1][1]
-    rows = (count + 2) * owned
+    rows = (count + 3) * owned
     joined = pl.pallas_call(
         functools.partial(join_body, owned, places, count),
-        in_specs=[vmem] * 6,
+        in_specs=[vmem] * 8,
         out_specs=vmem,
         out_shape=pltpu.VMEM((places * rows, LANES), F32),
-        scratch_shapes=[pltpu.VMEM((places * n * owned, LANES), F32) for n in (1, 1, count)],
+        scratch_shapes=[pltpu.VMEM((places * n * owned, LANES), F32) for n in (1, 1, 1, count)],
         compiler_params=params,
         name="join_rows",
-    )(z_keep, z_other, x_keep, x_other, keep, other)
+    )(z_keep, z_other, x_keep, x_other, y_keep, y_other, keep, other)
     tile = joined.reshape(places, rows, 1, LANES)
     got = lax.all_to_all(tile, ("zl", "x", "zh", "y"), split_axis=0, concat_axis=0, tiled=True)
     total = pl.pallas_call(

time: 55.4 us -> 58.4 us (1.054)
  blocking collectives: 30.3 us -> 27.4 us
  waiting for transfers between devices: 0.02 us -> 2.75 us
  starting transfers between devices: 3.73 us -> 5.75 us
  Pallas kernels: 21.1 us -> 22.3 us
    pallas_call x1, Pallas kernels: 9.14 us -> 12.2 us  [local(): pl.pallas_call(functools.partial(first_body, dims, geometry, chunks), in_...]
    all_to_all x1, blocking collectives: 30.3 us -> 27.4 us  [local(): lax.all_to_all(tile, ('zl', 'x', 'zh', 'y'), split_axis=0, concat_axis=0,...]
    ppermute x0 -> x1, waiting for transfers between devices: none -> 2.42 us  [local(): y_other = lax.ppermute(y_send, 'x', [(0, 3), (3, 0), (1, 2), (2, 1)])]
    pallas_call x1, Pallas kernels: 6.21 us -> 3.8 us  [local(): pl.pallas_call(functools.partial(next_body, geometry, chunks[1]), in_spec...]
    ppermute x0 -> x1, starting transfers between devices: none -> 2.1 us  [local(): y_other = lax.ppermute(y_send, 'x', [(0, 3), (3, 0), (1, 2), (2, 1)])]
  transfers between devices with their start and end apart: 4 -> 5, of which waited for: 0 -> 2; matrix products, arithmetic and copies ran while one was open for 0% -> 0% of each run, Pallas kernels for 20% -> 15%
where the time goes in v6:
time: 58.4 us; the launch traced here: 58.2 us
  blocking collectives  27.4 us (47%)
  Pallas kernels  22.3 us (38%)
  starting transfers between devices  5.75 us (10%)
  waiting for transfers between devices  2.75 us (5%)
    all_to_all x1, blocking collectives, local(): lax.all_to_all(tile, ('zl', 'x', 'zh', 'y'), split_axis=0, concat_axis=0,...  27.4 us
    pallas_call x1, Pallas kernels, local(): pl.pallas_call(functools.partial(first_body, dims, geometry, chunks), in_...  12.2 us
    pallas_call x2, Pallas kernels, own_part(): pl.pallas_call(functools.partial(own_body, geometry, chunks[n]), in_specs...  5.13 us
    pallas_call x1, Pallas kernels, local(): pl.pallas_call(functools.partial(next_body, geometry, chunks[1]), in_spec...  3.8 us
    ppermute x1, waiting for transfers between devices, local(): y_other = lax.ppermute(y_send, 'x', [(0, 3), (3, 0), (1, 2), (2, 1)])  2.42 us
    ppermute x1, starting transfers between devices, local(): y_other = lax.ppermute(y_send, 'x', [(0, 3), (3, 0), (1, 2), (2, 1)])  2.1 us
    ppermute x1, starting transfers between devices, local(): z_other = lax.ppermute(z_send, 'zl', swap)  2.08 us
    ppermute x1, starting transfers between devices, local(): x_other = lax.ppermute(x_send, 'x', [(0, 1), (1, 0), (2, 3), (3, 2)])  1.49 us
  transfers between devices with their start and end apart: 5, of which 2 were waited for; matrix products, arithmetic and copies ran while one was open for 0% of the time, Pallas kernels for 15%

profile of v6, /device:TPU:0, one launch (start us, length us, event | category | flops | bytes accessed | tf_op | source)
XLA Modules:
  0.0 58.2 jit_solution(9520540206646527203)
XLA Ops:
  0.0 0.0 copy-start
  0.0 12.2 %first_chunk.1 = (f32[2688,128]{1,0:T(8,128)S(1)}, f32[1024,896]{1,0:T(8,128)S(1)}, f32[6,1792,128]{2,1,0:T(8,128)S(1)}, bf16[16,112,2048]{2,1,0:T(8,128)(2,1)S(1)}, bf16[2048,896]{1,0:T(8,128)(2,1)S(1)}) custom-call(s32[112]{0:T(128)} %l_atom.5, f32[8]{0:T(128)} %kg_hbm.1, s32[1,112]{1,0:T(1,128)} %bitcast.14, f32[512,12]{1,0:T(8,128)} %bitcast.13, ...), custom_call_target="tpu_custom_call" | custom-call | tf_op jit(solution)/shard_map/first_chunk/pallas_call | solution.py:241
  12.2 0.1 collective-permute-start
  12.3 0.0 copy-done
  12.3 3.5 %own_part.2.keep_ref = f32[2688,128]{1,0:T(8,128)S(1)} custom-call(s32[112]{0:T(128)S(1)} %copy-done, f32[1024,896]{1,0:T(8,128)S(1)} %get-tuple-element.23.w_ref, f32[6,1792,128]{2,1,0:T(8,128)S(1)} %get-tuple-element.24.i_ref), custom_call_target="tpu_custom_call" | custom-call | tf_op jit(solution)/shard_map/own_part/pallas_call | solution.py:267
  15.9 0.0 collective-permute-done.other_ref
  15.9 0.2 split_tiles.1
  16.0 2.1 %collective-permute-start.1 = (f32[448,128]{1,0:T(8,128)S(1)}, f32[448,128]{1,0:T(8,128)S(1)}, u32[]{:S(2)}, u32[]{:S(2)}) collective-permute-start(f32[448,128]{1,0:T(8,128)S(1)} %get-tuple-element.31), channel_id=1, source_target_pairs={{0,64},{64,0},{1,65},{65,1},{2,66},{66,2},{3,67},{67,3},{4,68},{68... | collective-permute-start | bytes 688136 | tf_op jit(solution)/shard_map/ppermute | solution.py:288
  18.1 1.5 %collective-permute-start.2 = (f32[448,128]{1,0:T(8,128)S(1)}, f32[448,128]{1,0:T(8,128)S(1)}, u32[]{:S(2)}, u32[]{:S(2)}) collective-permute-start(f32[448,128]{1,0:T(8,128)S(1)} %get-tuple-element.32), channel_id=1, source_target_pairs={{0,16},{16,0},{32,48},{48,32},{1,17},{17,1},{33,49},{49,33},{2,18}... | collective-permute-start | bytes 688136 | tf_op jit(solution)/shard_map/ppermute | solution.py:289
  19.6 2.1 %collective-permute-start.3 = (f32[448,128]{1,0:T(8,128)S(1)}, f32[448,128]{1,0:T(8,128)S(1)}, u32[]{:S(2)}, u32[]{:S(2)}) collective-permute-start(f32[448,128]{1,0:T(8,128)S(1)} %get-tuple-element.33), channel_id=1, source_target_pairs={{0,48},{48,0},{16,32},{32,16},{1,49},{49,1},{17,33},{33,17},{2,50}... | collective-permute-start | bytes 688136 | tf_op jit(solution)/shard_map/ppermute | solution.py:290
  21.7 3.8 %next_chunk.1 = (f32[448,128]{1,0:T(8,128)S(1)}, f32[1,1792,128]{2,1,0:T(8,128)S(1)}) custom-call(s32[112]{0:T(128)S(1)} %copy-done, f32[1024,896]{1,0:T(8,128)S(1)} %get-tuple-element.23.w_ref, bf16[16,112,2048]{2,1,0:T(8,128)(2,1)S(1)} %get-tuple-element.27.a_ref, bf16[2048,896]{1,0:T(8,128)(2,1)S(1)} %get-tuple-element.28.ps_ref, ...), custom_call_target="tpu_custom_call" | custom-call | tf_op jit(solution)/shard_map/next_chunk/pallas_call | solution.py:291
  25.5 0.0 collective-permute-done.1.zo_ref
  25.5 0.3 collective-permute-done.2.xo_ref
  25.8 2.4 %collective-permute-done.3.yo_ref = f32[448,128]{1,0:T(8,128)S(1)} collective-permute-done((f32[448,128]{1,0:T(8,128)S(1)}, f32[448,128]{1,0:T(8,128)S(1)}, u32[]{:S(2)}, u32[]{:S(2)}) %collective-permute-start.3) | collective-permute-done | bytes 229408 | tf_op jit(solution)/shard_map/ppermute | solution.py:290
  28.3 0.0 collective-permute-start.4
  28.3 1.6 %own_part.3.keep_ref = f32[448,128]{1,0:T(8,128)S(1)} custom-call(s32[112]{0:T(128)S(1)} %copy-done, f32[1024,896]{1,0:T(8,128)S(1)} %get-tuple-element.23.w_ref, f32[1,1792,128]{2,1,0:T(8,128)S(1)} %get-tuple-element.39.i_ref), custom_call_target="tpu_custom_call" | custom-call | tf_op jit(solution)/shard_map/own_part/pallas_call | solution.py:267
  29.9 0.0 collective-permute-done.4.other_ref
  29.9 0.2 join_rows.1
  30.1 27.4 %all_to_all.5 = f32[64,28,1,128]{3,2,1,0:T(1,128)S(1)} all-to-all(f32[64,28,1,128]{3,2,1,0:T(1,128)S(1)} %bitcast.11), channel_id=1, replica_groups=mesh['zl'=2,'x'=4,'core'=2,'zh'=2,'y'=4] {'zl','x','zh','y'}, dimensions={0} | all-to-all | bytes 1835008 | tf_op jit(solution)/shard_map/all_to_all | solution.py:314
  57.5 0.7 %sum_sources.1 = f32[7,8,896]{2,1,0:T(8,128)} custom-call(f32[1792,128]{1,0:T(8,128)S(1)} %bitcast.10), custom_call_target="tpu_custom_call" | custom-call | tf_op jit(solution)/shard_map/sum_sources/pallas_call | solution.py:315
Async XLA Ops:
  0.0 12.3 %copy-start = (s32[112]{0:T(128)S(1)}, s32[112]{0:T(128)}, u32[]{:S(2)}) copy-start(s32[112]{0:T(128)} %l_atom.5) | copy-start | bytes 1348
  12.2 3.6 %collective-permute-start = (f32[2688,128]{1,0:T(8,128)S(1)}, f32[2688,128]{1,0:T(8,128)S(1)}, u32[]{:S(2)}, u32[]{:S(2)}) collective-permute-start(f32[2688,128]{1,0:T(8,128)S(1)} %get-tuple-element.25), channel_id=1, source_target_pairs={{0,8},{8,0},{1,9},{9,1},{2,10},{10,2},{3,11},{11,3},{4,12},{12,4},... | collective-permute-start | bytes 4128776 | tf_op jit(solution)/shard_map/ppermute | solution.py:278
  16.0 9.5 %collective-permute-start.1 = (f32[448,128]{1,0:T(8,128)S(1)}, f32[448,128]{1,0:T(8,128)S(1)}, u32[]{:S(2)}, u32[]{:S(2)}) collective-permute-start(f32[448,128]{1,0:T(8,128)S(1)} %get-tuple-element.31), channel_id=1, source_target_pairs={{0,64},{64,0},{1,65},{65,1},{2,66},{66,2},{3,67},{67,3},{4,68},{68... | collective-permute-start | bytes 688136 | tf_op jit(solution)/shard_map/ppermute | solution.py:288
  18.1 7.7 %collective-permute-start.2 = (f32[448,128]{1,0:T(8,128)S(1)}, f32[448,128]{1,0:T(8,128)S(1)}, u32[]{:S(2)}, u32[]{:S(2)}) collective-permute-start(f32[448,128]{1,0:T(8,128)S(1)} %get-tuple-element.32), channel_id=1, source_target_pairs={{0,16},{16,0},{32,48},{48,32},{1,17},{17,1},{33,49},{49,33},{2,18}... | collective-permute-start | bytes 688136 | tf_op jit(solution)/shard_map/ppermute | solution.py:289
  19.6 8.7 %collective-permute-start.3 = (f32[448,128]{1,0:T(8,128)S(1)}, f32[448,128]{1,0:T(8,128)S(1)}, u32[]{:S(2)}, u32[]{:S(2)}) collective-permute-start(f32[448,128]{1,0:T(8,128)S(1)} %get-tuple-element.33), channel_id=1, source_target_pairs={{0,48},{48,0},{16,32},{32,16},{1,49},{49,1},{17,33},{33,17},{2,50}... | collective-permute-start | bytes 688136 | tf_op jit(solution)/shard_map/ppermute | solution.py:290
  28.3 1.6 %collective-permute-start.4 = (f32[448,128]{1,0:T(8,128)S(1)}, f32[448,128]{1,0:T(8,128)S(1)}, u32[]{:S(2)}, u32[]{:S(2)}) collective-permute-start(f32[448,128]{1,0:T(8,128)S(1)} %get-tuple-element.40), channel_id=1, source_target_pairs={{0,8},{8,0},{1,9},{9,1},{2,10},{10,2},{3,11},{11,3},{4,12},{12,4},... | collective-permute-start | bytes 688136 | tf_op jit(solution)/shard_map/ppermute | solution.py:300

commit v7 on v5

--- a/solution.py
+++ b/solution.py
@@ -12,7 +12,7 @@
 BF16 = jnp.bfloat16
 LANES = 128
 SUB = 8
-FIRST = 4
+FIRST = 2
 BLOCK = 8
 VMEM_LIMIT = 28 * 1024 * 1024
 
@@ -168,23 +168,20 @@
     recouple(geometry, l_atom, i_ref, w_ref, keep_ref, chunk, lax.axis_index("core"))
 
 
-def split_body(rows, keep_ref, other_ref, z_keep_ref, z_send_ref, x_keep_ref, x_send_ref):
+def split_body(rows, keep_ref, other_ref, z_keep_ref, z_send_ref):
     z = lax.axis_index("zl")
-    x = lax.axis_index("x") % 2
-    for tile, out_ref in ((z, z_keep_ref), (1 - z, z_send_ref), (2 + x, x_keep_ref), (3 - x, x_send_ref)):
+    for tile, out_ref in ((z, z_keep_ref), (1 - z, z_send_ref)):
         at = pl.ds(pl.multiple_of(tile * rows, SUB), rows)
         out_ref[...] = keep_ref[at, :] + other_ref[at, :]
 
 
-def join_body(owned, places, count, zk_ref, zo_ref, xk_ref, xo_ref, keep_ref, other_ref, out_ref,
-              z_ref, x_ref, c_ref):
+def join_body(owned, places, count, zk_ref, zo_ref, keep_ref, other_ref, out_ref, z_ref, c_ref):
     z_ref[...] = zk_ref[...] + zo_ref[...]
-    x_ref[...] = xk_ref[...] + xo_ref[...]
     c_ref[...] = keep_ref[...] + other_ref[...]
-    rows = (count + 2) * owned
+    rows = (count + 1) * owned
 
     def group(d, carry):
-        for n, (ref, width) in enumerate(((z_ref, owned), (x_ref, owned), (c_ref, count * owned))):
+        for n, (ref, width) in enumerate(((z_ref, owned), (c_ref, count * owned))):
             for r in range(width):
                 part = ref[pl.ds(d * (SUB * width) + r, SUB, stride=width), :]
                 out_ref[pl.ds(d * (SUB * rows) + n * owned + r, SUB, stride=rows), :] = part
@@ -195,12 +192,12 @@
 
 def sum_body(owned, sources, total_j, chunks, got_ref, out_ref):
     first, count = chunks[0][1], chunks[1][1]
-    rows = (count + 2) * owned
+    rows = (count + 1) * owned
     everyone = list(range(sources))
     half = sources // 2
-    held = {0: (0, everyone[:half]), 1: (0, everyone[half:]), 2: (1, everyone[0::2]), 3: (1, everyone[1::2])}
+    held = {0: (0, everyone[:half]), 1: (0, everyone[half:])}
     for t in range(count):
-        held[first + t] = (2 + t, everyone)
+        held[first + t] = (1 + t, everyone)
     for r in range(owned):
         for t, (block, members) in held.items():
             acc = None
@@ -271,16 +268,15 @@
     swap = [(0, 1), (1, 0)]
     other = lax.ppermute(send, "core", swap)
     tile_part = pltpu.VMEM((places * owned, LANES), F32)
-    z_keep, z_send, x_keep, x_send = pl.pallas_call(
+    z_keep, z_send = pl.pallas_call(
         functools.partial(split_body, places * owned),
         in_specs=[vmem] * 2,
-        out_specs=[vmem] * 4,
-        out_shape=[tile_part] * 4,
+        out_specs=[vmem] * 2,
+        out_shape=[tile_part] * 2,
         compiler_params=params,
         name="split_tiles",
     )(own_part(0, product), other)
     z_other = lax.ppermute(z_send, "zl", swap)
-    x_other = lax.ppermute(x_send, "x", [(0, 1), (1, 0), (2, 3), (3, 2)])
     send, product = pl.pallas_call(
         functools.partial(next_body, geometry, chunks[1]),
         in_specs=[smem, vmem, vmem, vmem, pl.BlockSpec(memory_space=pl.ANY)],
@@ -289,20 +285,20 @@
         compiler_params=params,
         name="next_chunk",
     )(l_atom, table, left, right, z_keep)
-    send, product, z_other, x_other = lax.optimization_barrier((send, product, z_other, x_other))
+    send, product, z_other = lax.optimization_barrier((send, product, z_other))
     other = lax.ppermute(send, "core", swap)
     keep = own_part(1, product)
     count = chunks[1][1]
-    rows = (count + 2) * owned
+    rows = (count + 1) * owned
     joined = pl.pallas_call(
         functools.partial(join_body, owned, places, count),
-        in_specs=[vmem] * 6,
+        in_specs=[vmem] * 4,
         out_specs=vmem,
         out_shape=pltpu.VMEM((places * rows, LANES), F32),
-        scratch_shapes=[pltpu.VMEM((places * n * owned, LANES), F32) for n in (1, 1, count)],
+        scratch_shapes=[pltpu.VMEM((places * n * owned, LANES), F32) for n in (1, count)],
         compiler_params=params,
         name="join_rows",
-    )(z_keep, z_other, x_keep, x_other, keep, other)
+    )(z_keep, z_other, keep, other)
     tile = joined.reshape(places, rows, 1, LANES)
     got = lax.all_to_all(tile, ("zl", "x", "zh", "y"), split_axis=0, concat_axis=0, tiled=True)
     total = pl.pallas_call(

time: 55.4 us -> 57 us (1.029)
  blocking collectives: 30.3 us -> 32.7 us
  starting transfers between devices: 3.73 us -> 2.4 us
    pallas_call x1, Pallas kernels: 6.21 us -> 9.17 us  [local(): pl.pallas_call(functools.partial(next_body, geometry, chunks[1]), in_spec...]
    pallas_call x1, Pallas kernels: 9.14 us -> 6.39 us  [local(): pl.pallas_call(functools.partial(first_body, dims, geometry, chunks), in_...]
    all_to_all x1, blocking collectives: 30.3 us -> 32.7 us  [local(): lax.all_to_all(tile, ('zl', 'x', 'zh', 'y'), split_axis=0, concat_axis=0,...]
    ppermute x1 -> x0, starting transfers between devices: 1.48 us -> none  [local(): x_other = lax.ppermute(x_send, 'x', [(0, 1), (1, 0), (2, 3), (3, 2)])]
  transfers between devices with their start and end apart: 4 -> 3, of which waited for: 0 -> 1; matrix products, arithmetic and copies ran while one was open for 0% -> 0% of each run, Pallas kernels for 20% -> 25%
where the time goes in v7:
time: 57 us; the launch traced here: 56.8 us
  blocking collectives  32.7 us (57%)
  Pallas kernels  21.5 us (38%)
  starting transfers between devices  2.4 us (4%)
    all_to_all x1, blocking collectives, local(): lax.all_to_all(tile, ('zl', 'x', 'zh', 'y'), split_axis=0, concat_axis=0,...  32.7 us
    pallas_call x1, Pallas kernels, local(): pl.pallas_call(functools.partial(next_body, geometry, chunks[1]), in_spec...  9.17 us
    pallas_call x1, Pallas kernels, local(): pl.pallas_call(functools.partial(first_body, dims, geometry, chunks), in_...  6.39 us
    pallas_call x2, Pallas kernels, own_part(): pl.pallas_call(functools.partial(own_body, geometry, chunks[n]), in_specs...  4.85 us
    ppermute x1, starting transfers between devices, local(): z_other = lax.ppermute(z_send, 'zl', swap)  2.08 us
  transfers between devices with their start and end apart: 3, of which 1 were waited for; matrix products, arithmetic and copies ran while one was open for 0% of the time, Pallas kernels for 25%

profile of v7, /device:TPU:0, one launch (start us, length us, event | category | flops | bytes accessed | tf_op | source)
XLA Modules:
  0.0 56.8 jit_solution(13877927421555189494)
XLA Ops:
  0.0 0.0 copy-start
  0.0 6.4 %first_chunk.1 = (f32[896,128]{1,0:T(8,128)S(1)}, f32[1024,896]{1,0:T(8,128)S(1)}, f32[2,1792,128]{2,1,0:T(8,128)S(1)}, bf16[16,112,2048]{2,1,0:T(8,128)(2,1)S(1)}, bf16[2048,896]{1,0:T(8,128)(2,1)S(1)}) custom-call(s32[112]{0:T(128)} %l_atom.5, f32[8]{0:T(128)} %kg_hbm.1, s32[1,112]{1,0:T(1,128)} %bitcast.14, f32[512,12]{1,0:T(8,128)} %bitcast.13, ...), custom_call_target="tpu_custom_call" | custom-call | tf_op jit(solution)/shard_map/first_chunk/pallas_call | solution.py:232
  6.4 0.1 collective-permute-start
  6.5 0.0 copy-done
  6.5 1.7 %own_part.2.keep_ref = f32[896,128]{1,0:T(8,128)S(1)} custom-call(s32[112]{0:T(128)S(1)} %copy-done, f32[1024,896]{1,0:T(8,128)S(1)} %get-tuple-element.17.w_ref, f32[2,1792,128]{2,1,0:T(8,128)S(1)} %get-tuple-element.18.i_ref), custom_call_target="tpu_custom_call" | custom-call | tf_op jit(solution)/shard_map/own_part/pallas_call | solution.py:258
  8.2 0.1 collective-permute-done.other_ref
  8.4 2.1 %collective-permute-start.1 = (f32[448,128]{1,0:T(8,128)S(1)}, f32[448,128]{1,0:T(8,128)S(1)}, u32[]{:S(2)}, u32[]{:S(2)}) collective-permute-start(f32[448,128]{1,0:T(8,128)S(1)} %get-tuple-element.25), channel_id=1, source_target_pairs={{0,64},{64,0},{1,65},{65,1},{2,66},{66,2},{3,67},{67,3},{4,68},{68... | collective-permute-start | bytes 688136 | tf_op jit(solution)/shard_map/ppermute | solution.py:279
  10.4 9.2 %next_chunk.1 = (f32[2240,128]{1,0:T(8,128)S(1)}, f32[5,1792,128]{2,1,0:T(8,128)S(1)}) custom-call(s32[112]{0:T(128)S(1)} %copy-done, f32[1024,896]{1,0:T(8,128)S(1)} %get-tuple-element.17.w_ref, bf16[16,112,2048]{2,1,0:T(8,128)(2,1)S(1)} %get-tuple-element.21.a_ref, bf16[2048,896]{1,0:T(8,128)(2,1)S(1)} %get-tuple-element.22.ps_ref, ...), custom_call_target="tpu_custom_call" | custom-call | tf_op jit(solution)/shard_map/next_chunk/pallas_call | solution.py:280
  19.6 0.0 collective-permute-done.1.zo_ref
  19.6 0.2 collective-permute-start.2
  19.8 3.2 %own_part.3.keep_ref = f32[2240,128]{1,0:T(8,128)S(1)} custom-call(s32[112]{0:T(128)S(1)} %copy-done, f32[1024,896]{1,0:T(8,128)S(1)} %get-tuple-element.17.w_ref, f32[5,1792,128]{2,1,0:T(8,128)S(1)} %get-tuple-element.27.i_ref), custom_call_target="tpu_custom_call" | custom-call | tf_op jit(solution)/shard_map/own_part/pallas_call | solution.py:258
  23.0 0.0 collective-permute-done.2.other_ref
  23.0 0.3 join_rows.1
  23.3 32.7 %all_to_all.5 = f32[64,42,1,128]{3,2,1,0:T(1,128)S(1)} all-to-all(f32[64,42,1,128]{3,2,1,0:T(1,128)S(1)} %bitcast.10), channel_id=1, replica_groups=mesh['zl'=2,'x'=4,'core'=2,'zh'=2,'y'=4] {'zl','x','zh','y'}, dimensions={0} | all-to-all | bytes 2752512 | tf_op jit(solution)/shard_map/all_to_all | solution.py:303
  56.1 0.7 %sum_sources.1 = f32[7,8,896]{2,1,0:T(8,128)} custom-call(f32[2688,128]{1,0:T(8,128)S(1)} %bitcast.11), custom_call_target="tpu_custom_call" | custom-call | tf_op jit(solution)/shard_map/sum_sources/pallas_call | solution.py:304
  (1 shorter events, 0.0 us)
Async XLA Ops:
  0.0 6.5 %copy-start = (s32[112]{0:T(128)S(1)}, s32[112]{0:T(128)}, u32[]{:S(2)}) copy-start(s32[112]{0:T(128)} %l_atom.5) | copy-start | bytes 1348
  6.4 1.9 %collective-permute-start = (f32[896,128]{1,0:T(8,128)S(1)}, f32[896,128]{1,0:T(8,128)S(1)}, u32[]{:S(2)}, u32[]{:S(2)}) collective-permute-start(f32[896,128]{1,0:T(8,128)S(1)} %get-tuple-element.19), channel_id=1, source_target_pairs={{0,8},{8,0},{1,9},{9,1},{2,10},{10,2},{3,11},{11,3},{4,12},{12,4},... | collective-permute-start | bytes 1376264 | tf_op jit(solution)/shard_map/ppermute | solution.py:269
  8.4 11.3 %collective-permute-start.1 = (f32[448,128]{1,0:T(8,128)S(1)}, f32[448,128]{1,0:T(8,128)S(1)}, u32[]{:S(2)}, u32[]{:S(2)}) collective-permute-start(f32[448,128]{1,0:T(8,128)S(1)} %get-tuple-element.25), channel_id=1, source_target_pairs={{0,64},{64,0},{1,65},{65,1},{2,66},{66,2},{3,67},{67,3},{4,68},{68... | collective-permute-start | bytes 688136 | tf_op jit(solution)/shard_map/ppermute | solution.py:279
  19.6 3.4 %collective-permute-start.2 = (f32[2240,128]{1,0:T(8,128)S(1)}, f32[2240,128]{1,0:T(8,128)S(1)}, u32[]{:S(2)}, u32[]{:S(2)}) collective-permute-start(f32[2240,128]{1,0:T(8,128)S(1)} %get-tuple-element.28), channel_id=1, source_target_pairs={{0,8},{8,0},{1,9},{9,1},{2,10},{10,2},{3,11},{11,3},{4,12},{12,4},... | collective-permute-start | bytes 3440648 | tf_op jit(solution)/shard_map/ppermute | solution.py:289
